TPU v7x, 128 devices: a whole 4x4x4 slice. The times are simulated.
128 devices in a mesh: fsdp: 8 (over z, y_hi), ctx: 4 (over y_lo, core), tp: 4 (over x).
Axes of the slice: x: 4, y: 4 (y_hi: 2, y_lo: 2; y = y_hi * 2 + y_lo), z: 4, core: 2. Of those that a mesh axis runs over, the one named last changes fastest.
Arguments:
- hidden_in: bfloat16 [16384, 1024], P(('fsdp', 'ctx', 'tp')), may hold values from -6 to 6
- segment_ids: int32 [8, 2048], P('fsdp'), may hold values from 0 to 3, never falling along the last dimension, each value on 1 to 1024 neighbouring positions
- norm_gain: float32 [1, 2, 1024], P(None, None, ('fsdp', 'ctx', 'tp')), may hold values from 0.5 to 1.5
- norm_bias: float32 [1, 2, 1024], P(None, None, ('fsdp', 'ctx', 'tp')), may hold values from -3 to 3
- w_qkv: bfloat16 [1, 3, 1024, 1024], P(None, None, ('fsdp', 'ctx'), 'tp'), may hold values from -3 to 3
- qv_bias: bfloat16 [1, 2, 16, 64], P(None, None, 'tp', ('fsdp', 'ctx')), may hold values from -3 to 3
- w_out: bfloat16 [1, 1024, 1024], P(None, ('fsdp', 'ctx'), 'tp'), may hold values from -0.5 to 0.5
- out_bias: float32 [1, 2, 1024], P(None, None, ('fsdp', 'ctx', 'tp')), may hold values from -3 to 3
- w_up: bfloat16 [1, 1024, 4096], P(None, ('fsdp', 'ctx'), 'tp'), may hold values from -0.1875 to 0.1875
- up_bias: bfloat16 [1, 16, 256], P(None, 'tp', ('fsdp', 'ctx')), may hold values from -3 to 3
- w_down: bfloat16 [1, 1024, 4096], P(None, ('fsdp', 'ctx'), 'tp'), may hold values from -0.09375 to 0.09375
- cotangent: float32 [16384, 1024], P(('fsdp', 'ctx', 'tp')), may hold values from -6 to 6
Outputs:
- hidden_out: float32 [16384, 1024], P(('fsdp', 'ctx', 'tp'))
- hidden_grad: float32 [16384, 1024], P(('fsdp', 'ctx', 'tp'))
- norm_gain_grad: float32 [1, 2, 1024], P(None, None, ('fsdp', 'ctx', 'tp'))
- norm_bias_grad: float32 [1, 2, 1024], P(None, None, ('fsdp', 'ctx', 'tp'))
- w_qkv_grad: float32 [1, 3, 1024, 1024], P(None, None, ('fsdp', 'ctx'), 'tp')
- qv_bias_grad: float32 [1, 2, 16, 64], P(None, None, 'tp', ('fsdp', 'ctx'))
- w_out_grad: float32 [1, 1024, 1024], P(None, ('fsdp', 'ctx'), 'tp')
- out_bias_grad: float32 [1, 2, 1024], P(None, None, ('fsdp', 'ctx', 'tp'))
- w_up_grad: float32 [1, 1024, 4096], P(None, ('fsdp', 'ctx'), 'tp')
- up_bias_grad: float32 [1, 16, 256], P(None, 'tp', ('fsdp', 'ctx'))
- w_down_grad: float32 [1, 1024, 4096], P(None, ('fsdp', 'ctx'), 'tp')
Inputs may be any that keep to these rules, and one draw needn't show every extreme that they name: `segment_ids`: in each group's row the ids never fall; each of the 4 sequences holds 1 to 1024 positions and one holds exactly 1024.
All inputs are finite; a program needn't handle non-finite values.
Results may differ from a plain program's by a relative error of at most 0.025.
Values may be sent and summed in bfloat16 or wider, within the bound.
A program may use at most 128 MiB of HBM per device.

v0:
```python
import math

import jax
import jax.numpy as jnp
from jax import lax
from jax.sharding import PartitionSpec as P

H = 16
HD = 64


EPS = 1e-05
ROOT = 0.7978845608028654
CUBIC = 0.044715
CONTRACT_ROWS = (((0,), (0,)), ((), ()))
CONTRACT_COLS = (((1,), (1,)), ((), ()))


def normalize(residual, norm_gain, norm_shift):
    average = jnp.mean(residual, axis=1, keepdims=True)
    centered = residual - average
    inv_std = lax.rsqrt(jnp.mean(centered * centered, axis=1, keepdims=True) + EPS)
    standard = centered * inv_std
    return (standard, inv_std, (standard * norm_gain + norm_shift).astype(jnp.bfloat16))


def normalize_back(grad_norm, standard, inv_std, norm_gain):
    scaled = grad_norm * norm_gain
    return inv_std * (
        scaled
        - jnp.mean(scaled, axis=1, keepdims=True)
        - standard * jnp.mean(scaled * standard, axis=1, keepdims=True)
    )


def gelu_pair(preact):
    curve = jnp.tanh(ROOT * (preact + CUBIC * preact * preact * preact))
    output = 0.5 * preact * (1.0 + curve)
    derivative = 0.5 * (1.0 + curve) + 0.5 * preact * (1.0 - curve * curve) * ROOT * (
        1.0 + 3.0 * CUBIC * preact * preact
    )
    return (output, derivative)


def block_height(total_rows):
    return min(total_rows, max(512, total_rows // 8))


def key_window(first_row, height, total_rows):
    longest = min(2048, total_rows // 2)
    start = max(0, first_row - longest + 1) // 128 * 128
    return (start, first_row + height)


def block_scores(block_q, keys_part, segments, slopes, first_row, key_first):
    height = block_q.shape[0]
    width = keys_part.shape[0]
    scores = jnp.einsum("qhd,khd->hqk", block_q, keys_part, preferred_element_type=jnp.float32) * (
        1.0 / math.sqrt(block_q.shape[2])
    )
    row_pos = first_row + jnp.arange(height, dtype=jnp.int32)
    col_pos = key_first + jnp.arange(width, dtype=jnp.int32)
    distance = (row_pos[:, None] - col_pos[None, :]).astype(jnp.float32)
    row_seg = segments[first_row : first_row + height]
    col_seg = segments[key_first : key_first + width]
    allowed = (row_pos[:, None] >= col_pos[None, :]) & (row_seg[:, None] == col_seg[None, :])
    scores = scores - slopes[:, None, None] * distance[None, :, :]
    return jnp.where(allowed[None, :, :], scores, -jnp.inf)


def attend(queries, keys_all, values_all, segments, slopes):
    total_rows = queries.shape[0]
    height = block_height(total_rows)
    outputs = []
    sums = []
    for block_index in range(total_rows // height):
        first_row = block_index * height
        key_first, key_end = key_window(first_row, height, total_rows)
        block_q = queries[first_row : first_row + height]
        scores = block_scores(
            block_q, keys_all[key_first:key_end], segments, slopes, first_row, key_first
        )
        highest = jnp.max(scores, axis=2, keepdims=True)
        exponent = jnp.exp(scores - highest)
        totals = jnp.sum(exponent, axis=2, keepdims=True)
        attention = (exponent / totals).astype(jnp.bfloat16)
        outputs.append(
            jnp.einsum(
                "hqk,khd->qhd",
                attention,
                values_all[key_first:key_end],
                preferred_element_type=jnp.float32,
            ).astype(jnp.bfloat16)
        )
        sums.append((highest + jnp.log(totals))[:, :, 0])
    return (jnp.concatenate(outputs, axis=0), jnp.stack(sums))


def attend_back(queries, keys_all, values_all, grad_mixed, log_sums, segments, slopes):
    total_rows = queries.shape[0]
    height = block_height(total_rows)
    scale = 1.0 / math.sqrt(queries.shape[2])
    grad_keys = jnp.zeros(queries.shape, jnp.float32)
    grad_values = jnp.zeros(queries.shape, jnp.float32)
    query_parts = []
    for block_index in range(total_rows // height):
        first_row = block_index * height
        key_first, key_end = key_window(first_row, height, total_rows)
        block_q = queries[first_row : first_row + height]
        block_g = grad_mixed[first_row : first_row + height]
        keys_part = keys_all[key_first:key_end]
        values_part = values_all[key_first:key_end]
        scores = block_scores(block_q, keys_part, segments, slopes, first_row, key_first)
        attention = jnp.exp(scores - log_sums[block_index][:, :, None])
        grad_values = grad_values.at[key_first:key_end].add(
            jnp.einsum(
                "hqk,qhd->khd",
                attention.astype(jnp.bfloat16),
                block_g,
                preferred_element_type=jnp.float32,
            )
        )
        grad_attn = jnp.einsum(
            "qhd,khd->hqk", block_g, values_part, preferred_element_type=jnp.float32
        )
        centre = jnp.sum(attention * grad_attn, axis=2, keepdims=True)
        grad_scores = (attention * (grad_attn - centre) * scale).astype(jnp.bfloat16)
        query_parts.append(
            jnp.einsum(
                "hqk,khd->qhd", grad_scores, keys_part, preferred_element_type=jnp.float32
            ).astype(jnp.bfloat16)
        )
        grad_keys = grad_keys.at[key_first:key_end].add(
            jnp.einsum("hqk,qhd->khd", grad_scores, block_q, preferred_element_type=jnp.float32)
        )
    return (
        jnp.concatenate(query_parts, axis=0),
        grad_keys.astype(jnp.bfloat16),
        grad_values.astype(jnp.bfloat16),
    )


def on_device(
    hidden_in,
    segment_ids,
    norm_gain,
    norm_bias,
    w_qkv,
    qv_bias,
    w_out,
    out_bias,
    w_up,
    up_bias,
    w_down,
    cotangent,
):
    layer_count = w_qkv.shape[0]
    all_gains, all_shifts, all_biases = (
        lax.all_gather(norm_gain, ("fsdp", "ctx", "tp"), axis=2, tiled=True),
        lax.all_gather(norm_bias, ("fsdp", "ctx", "tp"), axis=2, tiled=True),
        lax.all_gather(out_bias, ("fsdp", "ctx", "tp"), axis=2, tiled=True),
    )
    segments = segment_ids[0]
    local_heads = H // lax.axis_size("tp") // lax.axis_size("ctx")
    head_first = (
        lax.axis_index("tp") * (H // lax.axis_size("tp")) + lax.axis_index("ctx") * local_heads
    )
    slopes = jnp.exp2(
        -8.0 * (head_first + jnp.arange(local_heads, dtype=jnp.int32) + 1).astype(jnp.float32) / H
    )

    def fetch(layer_index):
        return (
            lax.all_gather(w_qkv[layer_index], ("fsdp", "ctx"), axis=1, tiled=True),
            lax.all_gather(w_out[layer_index], ("fsdp", "ctx"), axis=0, tiled=True),
            lax.all_gather(w_up[layer_index], ("fsdp", "ctx"), axis=0, tiled=True),
            lax.all_gather(w_down[layer_index], ("fsdp", "ctx"), axis=0, tiled=True),
            lax.all_gather(qv_bias[layer_index], ("fsdp", "ctx"), axis=2, tiled=True),
            lax.all_gather(up_bias[layer_index], ("fsdp", "ctx"), axis=1, tiled=True),
        )

    def rows_all(local_rows):
        return lax.all_gather(local_rows, "tp", axis=0, tiled=True)

    def rows_sum(partial_sum):
        return lax.psum_scatter(
            partial_sum.astype(jnp.bfloat16), "tp", scatter_dimension=0, tiled=True
        ).astype(jnp.float32)

    residual = hidden_in.astype(jnp.float32)
    fetched = []
    layer_index = 0
    weights = fetch(layer_index)
    fetched.append(weights)
    mat_qkv, mat_out, mat_up, mat_down, bias_qv, bias_up = weights
    standard_attn, inv_attn, normed_attn = normalize(
        residual, all_gains[layer_index, 0], all_shifts[layer_index, 0]
    )
    wide_attn = rows_all(normed_attn)
    qv_add = bias_qv.astype(jnp.float32).reshape(2, -1)
    queries = (
        jnp.dot(wide_attn, mat_qkv[0], preferred_element_type=jnp.float32) + qv_add[0]
    ).astype(jnp.bfloat16)
    keys_row = jnp.dot(wide_attn, mat_qkv[1], preferred_element_type=jnp.float32).astype(
        jnp.bfloat16
    )
    values_row = (
        jnp.dot(wide_attn, mat_qkv[2], preferred_element_type=jnp.float32) + qv_add[1]
    ).astype(jnp.bfloat16)
    head_q = lax.all_to_all(queries, "ctx", split_axis=1, concat_axis=0, tiled=True)
    head_k = lax.all_to_all(keys_row, "ctx", split_axis=1, concat_axis=0, tiled=True)
    head_v = lax.all_to_all(values_row, "ctx", split_axis=1, concat_axis=0, tiled=True)
    head_shape = (head_q.shape[0], local_heads, HD)
    head_q = head_q.reshape(head_shape)
    head_k = head_k.reshape(head_shape)
    head_v = head_v.reshape(head_shape)
    head_out, log_sums = attend(head_q, head_k, head_v, segments, slopes)
    mixed = lax.all_to_all(
        head_out.reshape(head_shape[0], -1), "ctx", split_axis=0, concat_axis=1, tiled=True
    )
    residual_mid = (
        residual
        + rows_sum(
            lax.dot_general(mixed, mat_out, CONTRACT_COLS, preferred_element_type=jnp.float32)
        )
        + all_biases[layer_index, 0]
    )
    standard_mlp, inv_mlp, normed_mlp = normalize(
        residual_mid, all_gains[layer_index, 1], all_shifts[layer_index, 1]
    )
    wide_mlp = rows_all(normed_mlp)
    preact = jnp.dot(wide_mlp, mat_up, preferred_element_type=jnp.float32) + bias_up.astype(
        jnp.float32
    ).reshape(-1)
    activated, derivative = gelu_pair(preact)
    activated = activated.astype(jnp.bfloat16)
    residual_out = (
        residual_mid
        + rows_sum(
            lax.dot_general(activated, mat_down, CONTRACT_COLS, preferred_element_type=jnp.float32)
        )
        + all_biases[layer_index, 1]
    )
    saved = (
        standard_attn,
        inv_attn,
        wide_attn,
        head_q,
        head_k,
        head_v,
        log_sums,
        mixed,
        standard_mlp,
        inv_mlp,
        wide_mlp,
        derivative,
        activated,
    )
    residual, saved = (residual_out, saved)
    stored = [saved]
    gradient = cotangent
    matrix_parts = [None] * layer_count
    gain_parts = [None] * layer_count
    shift_parts = [None] * layer_count
    bias_parts = [None] * layer_count
    for layer_index in reversed(range(layer_count)):
        weights = fetch(layer_index)
        backward_saved = stored[layer_index]
        (
            backward_mat_qkv,
            backward_mat_out,
            backward_mat_up,
            backward_mat_down,
            backward_bias_qv,
            backward_bias_up,
        ) = weights
        (
            backward_standard_attn,
            backward_inv_attn,
            backward_wide_attn,
            backward_head_q,
            backward_head_k,
            backward_head_v,
            backward_log_sums,
            backward_mixed,
            backward_standard_mlp,
            backward_inv_mlp,
            backward_wide_mlp,
            backward_derivative,
            backward_activated,
        ) = backward_saved
        down_bias_grad = jnp.sum(gradient, axis=0)
        grad_wide = rows_all(gradient.astype(jnp.bfloat16))
        grad_down = lax.dot_general(
            grad_wide, backward_activated, CONTRACT_ROWS, preferred_element_type=jnp.float32
        )
        grad_pre = (
            jnp.dot(grad_wide, backward_mat_down, preferred_element_type=jnp.float32)
            * backward_derivative
        )
        up_bias_grad = jnp.sum(grad_pre, axis=0).reshape(backward_bias_up.shape)
        grad_pre16 = grad_pre.astype(jnp.bfloat16)
        grad_up = lax.dot_general(
            backward_wide_mlp, grad_pre16, CONTRACT_ROWS, preferred_element_type=jnp.float32
        )
        grad_norm = rows_sum(
            lax.dot_general(
                grad_pre16, backward_mat_up, CONTRACT_COLS, preferred_element_type=jnp.float32
            )
        )
        gain_mlp = jnp.sum(grad_norm * backward_standard_mlp, axis=0)
        shift_mlp = jnp.sum(grad_norm, axis=0)
        grad_mid = gradient + normalize_back(
            grad_norm, backward_standard_mlp, backward_inv_mlp, all_gains[layer_index, 1]
        )
        attn_bias_grad = jnp.sum(grad_mid, axis=0)
        grad_attn = rows_all(grad_mid.astype(jnp.bfloat16))
        grad_wout = lax.dot_general(
            grad_attn, backward_mixed, CONTRACT_ROWS, preferred_element_type=jnp.float32
        )
        grad_mixed = jnp.dot(
            grad_attn, backward_mat_out, preferred_element_type=jnp.float32
        ).astype(jnp.bfloat16)
        grad_heads = lax.all_to_all(
            grad_mixed, "ctx", split_axis=1, concat_axis=0, tiled=True
        ).reshape(backward_head_q.shape)
        grad_q, grad_k, grad_v = attend_back(
            backward_head_q,
            backward_head_k,
            backward_head_v,
            grad_heads,
            backward_log_sums,
            segments,
            slopes,
        )
        flat_rows = backward_head_q.shape[0]
        rows_q = lax.all_to_all(
            grad_q.reshape(flat_rows, -1), "ctx", split_axis=0, concat_axis=1, tiled=True
        )
        rows_k = lax.all_to_all(
            grad_k.reshape(flat_rows, -1), "ctx", split_axis=0, concat_axis=1, tiled=True
        )
        rows_v = lax.all_to_all(
            grad_v.reshape(flat_rows, -1), "ctx", split_axis=0, concat_axis=1, tiled=True
        )
        qv_grad = jnp.stack(
            [
                jnp.sum(rows_q.astype(jnp.float32), axis=0),
                jnp.sum(rows_v.astype(jnp.float32), axis=0),
            ]
        ).reshape(backward_bias_qv.shape)
        grad_qkv = jnp.stack(
            [
                lax.dot_general(
                    backward_wide_attn, rows_q, CONTRACT_ROWS, preferred_element_type=jnp.float32
                ),
                lax.dot_general(
                    backward_wide_attn, rows_k, CONTRACT_ROWS, preferred_element_type=jnp.float32
                ),
                lax.dot_general(
                    backward_wide_attn, rows_v, CONTRACT_ROWS, preferred_element_type=jnp.float32
                ),
            ]
        )
        back_terms = (
            lax.dot_general(
                rows_q, backward_mat_qkv[0], CONTRACT_COLS, preferred_element_type=jnp.float32
            )
            + lax.dot_general(
                rows_k, backward_mat_qkv[1], CONTRACT_COLS, preferred_element_type=jnp.float32
            )
            + lax.dot_general(
                rows_v, backward_mat_qkv[2], CONTRACT_COLS, preferred_element_type=jnp.float32
            )
        )
        grad_norm = rows_sum(back_terms)
        gain_attn = jnp.sum(grad_norm * backward_standard_attn, axis=0)
        shift_attn = jnp.sum(grad_norm, axis=0)
        grad_input = grad_mid + normalize_back(
            grad_norm, backward_standard_attn, backward_inv_attn, all_gains[layer_index, 0]
        )
        matrices = (grad_qkv, grad_wout, grad_up, grad_down, qv_grad, up_bias_grad)
        (
            gradient,
            matrices,
            gain_parts[layer_index],
            shift_parts[layer_index],
            bias_parts[layer_index],
        ) = (
            grad_input,
            matrices,
            jnp.stack([gain_attn, gain_mlp]),
            jnp.stack([shift_attn, shift_mlp]),
            jnp.stack([attn_bias_grad, down_bias_grad]),
        )
        matrix_parts[layer_index] = (
            lax.psum_scatter(
                matrices[0].astype(jnp.bfloat16), ("fsdp", "ctx"), scatter_dimension=1, tiled=True
            ).astype(jnp.float32),
            lax.psum_scatter(
                matrices[1].astype(jnp.bfloat16), ("fsdp", "ctx"), scatter_dimension=0, tiled=True
            ).astype(jnp.float32),
            lax.psum_scatter(
                matrices[2].astype(jnp.bfloat16), ("fsdp", "ctx"), scatter_dimension=0, tiled=True
            ).astype(jnp.float32),
            lax.psum_scatter(
                matrices[3].astype(jnp.bfloat16), ("fsdp", "ctx"), scatter_dimension=0, tiled=True
            ).astype(jnp.float32),
            lax.psum_scatter(
                matrices[4].astype(jnp.bfloat16), ("fsdp", "ctx"), scatter_dimension=2, tiled=True
            ).astype(jnp.float32),
            lax.psum_scatter(
                matrices[5].astype(jnp.bfloat16), ("fsdp", "ctx"), scatter_dimension=1, tiled=True
            ).astype(jnp.float32),
        )
    stacked = [jnp.stack([matrix_parts[0][member]]) for member in range(6)]
    gain_grads = jnp.stack(gain_parts)
    shift_grads = jnp.stack(shift_parts)
    bias_grads = jnp.stack(bias_parts)
    summed_gains, summed_shifts, summed_biases = (
        lax.psum_scatter(gain_grads, ("fsdp", "ctx", "tp"), scatter_dimension=2, tiled=True),
        lax.psum_scatter(shift_grads, ("fsdp", "ctx", "tp"), scatter_dimension=2, tiled=True),
        lax.psum_scatter(bias_grads, ("fsdp", "ctx", "tp"), scatter_dimension=2, tiled=True),
    )
    return (
        residual,
        gradient,
        summed_gains,
        summed_shifts,
        stacked[0],
        stacked[4],
        stacked[1],
        summed_biases,
        stacked[2],
        stacked[5],
        stacked[3],
    )


def solution(mesh):
    return jax.shard_map(
        on_device,
        mesh=mesh,
        in_specs=(
            P(("fsdp", "ctx", "tp"), None),
            P("fsdp", None),
            P(None, None, ("fsdp", "ctx", "tp")),
            P(None, None, ("fsdp", "ctx", "tp")),
            P(None, None, ("fsdp", "ctx"), "tp"),
            P(None, None, "tp", ("fsdp", "ctx")),
            P(None, ("fsdp", "ctx"), "tp"),
            P(None, None, ("fsdp", "ctx", "tp")),
            P(None, ("fsdp", "ctx"), "tp"),
            P(None, "tp", ("fsdp", "ctx")),
            P(None, ("fsdp", "ctx"), "tp"),
            P(("fsdp", "ctx", "tp"), None),
        ),
        out_specs=(
            P(("fsdp", "ctx", "tp"), None),
            P(("fsdp", "ctx", "tp"), None),
            P(None, None, ("fsdp", "ctx", "tp")),
            P(None, None, ("fsdp", "ctx", "tp")),
            P(None, None, ("fsdp", "ctx"), "tp"),
            P(None, None, "tp", ("fsdp", "ctx")),
            P(None, ("fsdp", "ctx"), "tp"),
            P(None, None, ("fsdp", "ctx", "tp")),
            P(None, ("fsdp", "ctx"), "tp"),
            P(None, "tp", ("fsdp", "ctx")),
            P(None, ("fsdp", "ctx"), "tp"),
        ),
        check_vma=False,
    )
```

profile of v0, /device:TPU:1, one launch (start us, length us, event | category | flops | bytes accessed | tf_op | source)
XLA Modules:
  0.0 906.8 jit_solution(8034377951889432527)
XLA Ops:
  11.1 55.9 %all_gather.44 = f32[1,2,1024]{1,0,2:T(1,128)S(1)} all-gather(f32[1,2,8]{1,0,2:T(1,128)S(1)} %copy.86), channel_id=1, replica_groups=mesh['fsdp'=8,'ctx'=4,'tp'=4] {'fsdp','ctx','tp'}, dimensions={2}, use_global_device_ids=true | all-gather | bytes 8256 | tf_op jit(solution)/shard_map/all_gather | solution.py:160
  66.9 7.2 slice_reduce_fusion.4
  74.1 51.4 %all_gather.43 = f32[1,2,1024]{1,0,2:T(1,128)S(1)} all-gather(f32[1,2,8]{1,0,2:T(1,128)S(1)} %copy.85), channel_id=1, replica_groups=mesh['fsdp'=8,'ctx'=4,'tp'=4] {'fsdp','ctx','tp'}, dimensions={2}, use_global_device_ids=true | all-gather | bytes 8256 | tf_op jit(solution)/shard_map/all_gather | solution.py:159
  125.5 7.2 slice_reduce_fusion.5
  134.5 22.6 %all-gather.1 = bf16[1,2,4,64]{2,1,0,3:T(2,128)(2,1)S(1)} all-gather(bf16[1,2,4,2]{2,1,0,3:T(2,128)(2,1)S(1)} %copy.87), channel_id=3, replica_groups=mesh['fsdp'=8,'ctx'=4,'tp'=4] {'fsdp','ctx'}, dimensions={3}, use_global_device_ids=true | all-gather | bytes 1056 | tf_op jit(solution)/shard_map/all_gather | solution.py:178
  160.5 41.5 %all-gather.22.cloned.1.call-done = bf16[1,3,1024,256]{3,2,1,0:T(8,128)(2,1)} async-done(((bf16[1,3,32,256]{3,2,1,0:T(8,128)(2,1)}), bf16[1,3,1024,256]{3,2,1,0:T(8,128)(2,1)}) %all-gather.22.cloned.1.call-update) | async-done | bytes 1572880 | tf_op jit(solution)/shard_map/all_gather | solution.py:174
  202.0 2.5 convolution_convert_fusion.7
  204.6 3.6 all-to-all-start.2
  213.4 4.2 all-to-all-start
  217.7 5.1 all-to-all-done
  222.8 4.6 all-to-all-start.1
  247.7 4.9 all-to-all-start.3
  252.6 26.9 %all-gather.2 = bf16[1,1024,256]{2,1,0:T(8,128)(2,1)} all-gather(bf16[1,32,256]{2,1,0:T(8,128)(2,1)} %param.34), channel_id=4, replica_groups=mesh['fsdp'=8,'ctx'=4,'tp'=4] {'fsdp','ctx'}, dimensions={1}, use_global_device_ids=true | all-gather | bytes 540672 | tf_op jit(solution)/shard_map/all_gather | solution.py:175
  279.5 2.6 convolution_convert_fusion.1
  283.5 53.1 %all_gather.49 = f32[1,2,1024]{1,0,2:T(1,128)S(1)} all-gather(f32[1,2,8]{1,0,2:T(1,128)S(1)} %copy.97), channel_id=1, replica_groups=mesh['fsdp'=8,'ctx'=4,'tp'=4] {'fsdp','ctx','tp'}, dimensions={2}, use_global_device_ids=true | all-gather | bytes 8256 | tf_op jit(solution)/shard_map/all_gather | solution.py:161
  336.6 6.2 slice_reduce_fusion
  347.5 2.5 fusion.117
  351.6 25.1 %all-gather.4 = bf16[1,4,256]{1,0,2:T(2,128)(2,1)} all-gather(bf16[1,4,8]{1,0,2:T(2,128)(2,1)S(1)} %copy.98), channel_id=6, replica_groups=mesh['fsdp'=8,'ctx'=4,'tp'=4] {'fsdp','ctx'}, dimensions={2}, use_global_device_ids=true | all-gather | bytes 2112 | tf_op jit(solution)/shard_map/all_gather | solution.py:179
  377.8 4.5 fusion.29
  382.3 18.5 %all-gather.18.cloned.1.call-done = bf16[512,1024]{1,0:T(8,128)(2,1)} async-done(((bf16[128,1024]{1,0:T(8,128)(2,1)}), bf16[512,1024]{1,0:T(8,128)(2,1)}) %all-gather.18.cloned.1.call-update) | async-done | bytes 1048592 | tf_op jit(solution)/shard_map/all_gather | solution.py:183
  400.9 48.2 %all-gather.26.cloned.1.call-done = bf16[1,1024,1024]{2,1,0:T(8,128)(2,1)} async-done(((bf16[1,32,1024]{2,1,0:T(8,128)(2,1)}), bf16[1,1024,1024]{2,1,0:T(8,128)(2,1)}) %all-gather.26.cloned.1.call-update) | async-done | bytes 2097168 | tf_op jit(solution)/shard_map/all_gather | solution.py:177
  449.1 5.6 fusion.124
  458.3 4.7 fusion.43
  463.0 16.2 %reduce-scatter.20.cloned.1.call-done = bf16[128,1024]{1,0:T(8,128)(2,1)} async-done(((bf16[512,1024]{1,0:T(8,128)(2,1)}), bf16[128,1024]{1,0:T(8,128)(2,1)}) %reduce-scatter.20.cloned.1.call-update) | async-done | bytes 262160 | tf_op jit(solution)/shard_map/reduce_scatter | solution.py:186
  481.8 23.0 %reduce-scatter.18.cloned.1.call-done = bf16[128,1024]{1,0:T(8,128)(2,1)} async-done(((bf16[512,1024]{1,0:T(8,128)(2,1)}), bf16[128,1024]{1,0:T(8,128)(2,1)}) %reduce-scatter.18.cloned.1.call-update) | async-done | bytes 262160 | tf_op jit(solution)/shard_map/reduce_scatter | solution.py:186
  504.8 3.0 fusion.115
  509.4 5.0 convert_bitcast_fusion
  514.4 4.0 copy.115
  518.4 4.3 convolution_convert_fusion
  526.1 7.5 all-gather.20.cloned.1.call-done
  533.6 2.6 convolution_convert_fusion.6
  536.2 5.6 all-to-all-start.4
  541.8 2.6 convolution_convert_fusion.2
  544.4 2.7 all-to-all-done.4
  555.0 3.2 multiply_reduce_fusion.2
  560.2 3.8 multiply_reduce_fusion.1
  565.6 3.8 multiply_reduce_fusion
  576.2 2.9 multiply_convert_fusion.2
  587.2 4.3 all-to-all-start.5
  597.7 4.0 all-to-all-start.6
  603.3 3.6 all-to-all-done.6
  606.9 4.2 all-to-all-start.7
  611.2 2.9 fusion.105
  614.0 2.8 all-to-all-done.7
  616.8 3.3 add_convert_fusion
  626.3 72.5 %reduce-scatter.28.cloned.1.call-done = bf16[32,1024]{1,0:T(8,128)(2,1)} async-done(((bf16[1024,1024]{1,0:T(8,128)(2,1)}), bf16[32,1024]{1,0:T(8,128)(2,1)}) %reduce-scatter.28.cloned.1.call-update) | async-done | bytes 65552 | tf_op jit(solution)/shard_map/reduce_scatter | solution.py:403
  701.6 121.0 %all-reduce.8 = (bf16[2,4,64]{1,2,0:T(8,128)(2,1)S(1)}, bf16[4,256]{1,0:T(4,128)(2,1)S(1)}) all-reduce(bf16[2,4,64]{1,2,0:T(8,128)(2,1)S(1)} %copy.103, bf16[4,256]{1,0:T(4,128)(2,1)S(1)} %convert_element_type.309), channel_id=15, replica_groups=mesh['fsdp'=8,'ctx'=4,'tp'=4] {'fsdp','ctx'}, use_global_device_ids=true, to_apply=%region_33.34.clone | all-reduce | flops 1536 | bytes 6144
  826.4 68.0 %all-reduce.7 = (f32[1,2,1024]{2,1,0:T(2,128)S(1)}, f32[1,2,1024]{2,1,0:T(2,128)S(1)}, f32[1,2,1024]{2,1,0:T(2,128)S(1)}) all-reduce(f32[1,2,1024]{2,1,0:T(2,128)S(1)} %maximum_bitcast_fusion, f32[1,2,1024]{2,1,0:T(2,128)S(1)} %maximum_bitcast_fusion.1, ...), channel_id=12, replica_groups=mesh['fsdp'=8,'ctx'=4,'tp'=4] {'fsdp','ctx','tp'}, use_global_device_ids=true, to_apply=%region_26.27.clone | all-reduce | flops 6144 | bytes 49152
  (304 shorter events, 104.6 us)
Async XLA Ops:
  7.2 125.5 %copy-start.5 = (bf16[128,1024]{1,0:T(8,128)(2,1)S(1)}, bf16[128,1024]{1,0:T(8,128)(2,1)}, u32[]{:S(2)}) copy-start(bf16[128,1024]{1,0:T(8,128)(2,1)} %param.28) | copy-start | bytes 786436
  7.2 153.3 %all-gather.14.cloned.1.call-start = ((), (), s32[]{:S(2)}) async-start(), calls=%async_computation.16 | async-start | bytes 1310720 | tf_op jit(solution)/shard_map/all_gather | solution.py:183
  8.3 125.3 %copy-start.53 = (f32[128]{0:T(128)}, f32[128]{0:T(128)S(1)}, u32[]{:S(2)}) copy-start(f32[128]{0:T(128)S(1)} %broadcast_multiply_fusion.5) | copy-start | bytes 1540
  8.4 126.1 %copy-start.66 = (bf16[1,2,4,2]{2,3,1,0:T(2,128)(2,1)S(1)}, bf16[1,2,4,2]{2,3,1,0:T(2,128)(2,1)}, u32[]{:S(2)}) copy-start(bf16[1,2,4,2]{2,3,1,0:T(2,128)(2,1)} %param.33) | copy-start | bytes 100
  9.5 125.0 %copy-start.58 = (f32[128]{0:T(128)}, f32[128]{0:T(128)S(1)}, u32[]{:S(2)}) copy-start(f32[128]{0:T(128)S(1)} %add_rsqrt_fusion.1) | copy-start | bytes 1540
  11.1 148.3 %copy-start.33 = (s32[1,2048]{1,0:T(1,128)S(1)}, s32[1,2048]{1,0:T(1,128)}, u32[]{:S(2)}) copy-start(s32[1,2048]{1,0:T(1,128)} %param.29) | copy-start | bytes 24580
  133.7 68.3 %all-gather.22.cloned.1.call-start = ((), (), s32[]{:S(2)}) async-start(), calls=%async_computation.27 | async-start | bytes 1622016 | tf_op jit(solution)/shard_map/all_gather | solution.py:174
  160.5 47.6 %copy-start.12 = (bf16[512,1024]{1,0:T(8,128)(2,1)S(1)}, bf16[512,1024]{1,0:T(8,128)(2,1)}, u32[]{:S(2)}) copy-start(bf16[512,1024]{1,0:T(8,128)(2,1)} %all-gather.14.cloned.1.call-done) | copy-start | bytes 3145732
  204.6 8.8 all-to-all-start.2
  213.4 19.2 %copy-start.17 = (bf16[512,4,64]{0,2,1:T(8,128)(2,1)}, bf16[512,4,64]{0,2,1:T(8,128)(2,1)S(1)}, u32[]{:S(2)}) copy-start(bf16[512,4,64]{0,2,1:T(8,128)(2,1)S(1)} %all-to-all-done.2) | copy-start | bytes 786436
  213.4 9.4 %all-to-all-start = ((bf16[512,4,64]{0,2,1:T(8,128)(2,1)}), bf16[512,4,64]{0,2,1:T(8,128)(2,1)S(1)}, u32[]{:S(2)}, u32[]{:S(2)}) async-start(bf16[512,4,64]{0,2,1:T(8,128)(2,1)} %bitcast.1), calls=%async_computation | async-start | bytes 524288 | tf_op jit(solution)/shard_map/all_to_all | solution.py:212
  222.8 10.5 %copy-start.18 = (bf16[512,4,64]{0,2,1:T(8,128)(2,1)}, bf16[512,4,64]{0,2,1:T(8,128)(2,1)S(1)}, u32[]{:S(2)}) copy-start(bf16[512,4,64]{0,2,1:T(8,128)(2,1)S(1)} %all-to-all-done) | copy-start | bytes 786436
  222.8 9.8 %all-to-all-start.1 = ((bf16[512,4,64]{0,2,1:T(8,128)(2,1)}), bf16[512,4,64]{0,2,1:T(8,128)(2,1)S(1)}, u32[]{:S(2)}, u32[]{:S(2)}) async-start(bf16[512,4,64]{0,2,1:T(8,128)(2,1)} %bitcast.6), calls=%async_computation.1 | async-start | bytes 524288 | tf_op jit(solution)/shard_map/all_to_all | solution.py:210
  227.5 8.2 copy-start.30
  247.7 31.8 %all-to-all-start.3 = ((bf16[4,512,64]{1,2,0:T(8,128)(2,1)}), bf16[4,512,64]{1,2,0:T(8,128)(2,1)}, u32[]{:S(2)}, u32[]{:S(2)}) async-start(bf16[4,512,64]{1,2,0:T(8,128)(2,1)} %copy.96), calls=%async_computation.3 | async-start | bytes 524288 | tf_op jit(solution)/shard_map/all_to_all | solution.py:218
  252.6 90.1 %reduce-scatter.16.cloned.1.call-start = ((), (), s32[]{:S(2)}) async-start(), calls=%async_computation.17 | async-start | bytes 1310720 | tf_op jit(solution)/shard_map/reduce_scatter | solution.py:186
  282.1 95.7 %all-gather.24.cloned.1.call-start = ((), (), s32[]{:S(2)}) async-start(), calls=%async_computation.28 | async-start | bytes 2162688 | tf_op jit(solution)/shard_map/all_gather | solution.py:176
  282.7 95.1 %all-gather.16.cloned.1.call-start = ((), (), s32[]{:S(2)}) async-start(), calls=%async_computation.18 | async-start | bytes 1310720 | tf_op jit(solution)/shard_map/all_gather | solution.py:183
  347.4 53.5 %all-gather.18.cloned.1.call-start = ((), (), s32[]{:S(2)}) async-start(), calls=%async_computation.20 | async-start | bytes 1310720 | tf_op jit(solution)/shard_map/all_gather | solution.py:183
  350.0 99.0 %all-gather.26.cloned.1.call-start = ((), (), s32[]{:S(2)}) async-start(), calls=%async_computation.29 | async-start | bytes 2162688 | tf_op jit(solution)/shard_map/all_gather | solution.py:177
  350.8 128.5 %reduce-scatter.20.cloned.1.call-start = ((), (), s32[]{:S(2)}) async-start(), calls=%async_computation.21 | async-start | bytes 1310720 | tf_op jit(solution)/shard_map/reduce_scatter | solution.py:186
  377.7 71.3 %copy-start.60 = (f32[1,2,4,128]{3,1,2,0:T(2,128)}, f32[1,2,4,128]{3,1,2,0:T(2,128)S(1)}, u32[]{:S(2)}) copy-start(f32[1,2,4,128]{3,1,2,0:T(2,128)S(1)} %copy.123) | copy-start | bytes 12292
  449.1 6.6 copy-start.67
  458.0 46.8 %copy-start.34 = (f32[1024]{0:T(1024)S(1)}, f32[1024]{0:T(1024)}, u32[]{:S(2)}) copy-start(f32[1024]{0:T(1024)} %get-tuple-element.177) | copy-start | bytes 12292
  458.0 46.8 %reduce-scatter.18.cloned.1.call-start = ((), (), s32[]{:S(2)}) async-start(), calls=%async_computation.19 | async-start | bytes 1310720 | tf_op jit(solution)/shard_map/reduce_scatter | solution.py:186
  463.0 70.6 %all-gather.20.cloned.1.call-start = ((), (), s32[]{:S(2)}) async-start(), calls=%async_computation.22 | async-start | bytes 1310720 | tf_op jit(solution)/shard_map/all_gather | solution.py:183
  509.3 113.0 %reduce-scatter.30.cloned.1.call-start = ((), (), s32[]{:S(2)}) async-start(), calls=%async_computation.30 | async-start | bytes 2162688
  518.3 180.5 %reduce-scatter.28.cloned.1.call-start = ((), (), s32[]{:S(2)}) async-start(), calls=%async_computation.26 | async-start | bytes 2162688 | tf_op jit(solution)/shard_map/reduce_scatter | solution.py:403
  536.2 10.9 %all-to-all-start.4 = ((bf16[512,4,64]{0,2,1:T(8,128)(2,1)}), bf16[512,4,64]{0,2,1:T(8,128)(2,1)}, u32[]{:S(2)}, u32[]{:S(2)}) async-start(bf16[512,4,64]{0,2,1:T(8,128)(2,1)} %bitcast.351), calls=%async_computation.7 | async-start | bytes 524288 | tf_op jit(solution)/shard_map/all_to_all | solution.py:324
  541.8 282.0 %reduce-scatter.26.cloned.1.call-start = ((), (), s32[]{:S(2)}) async-start(), calls=%async_computation.25 | async-start | bytes 540672 | tf_op jit(solution)/shard_map/reduce_scatter | solution.py:400
  550.3 4.6 copy-start.4
  550.4 4.6 copy-start.31
  576.2 3.7 copy-start.11
  585.0 6.5 copy-start.9
  587.2 10.5 %all-to-all-start.5 = ((bf16[4,512,64]{1,2,0:T(8,128)(2,1)}), bf16[4,512,64]{1,2,0:T(8,128)(2,1)S(1)}, u32[]{:S(2)}, u32[]{:S(2)}) async-start(bf16[4,512,64]{1,2,0:T(8,128)(2,1)} %copy.100), calls=%async_computation.8 | async-start | bytes 524288 | tf_op jit(solution)/shard_map/all_to_all | solution.py:337
  597.7 9.2 %all-to-all-start.6 = ((bf16[4,512,64]{1,2,0:T(8,128)(2,1)}), bf16[4,512,64]{1,2,0:T(8,128)(2,1)S(1)}, u32[]{:S(2)}, u32[]{:S(2)}) async-start(bf16[4,512,64]{1,2,0:T(8,128)(2,1)} %copy.101), calls=%async_computation.9 | async-start | bytes 524288 | tf_op jit(solution)/shard_map/all_to_all | solution.py:340
  606.9 9.9 %all-to-all-start.7 = ((bf16[4,512,64]{1,2,0:T(8,128)(2,1)}), bf16[4,512,64]{1,2,0:T(8,128)(2,1)S(1)}, u32[]{:S(2)}, u32[]{:S(2)}) async-start(bf16[4,512,64]{1,2,0:T(8,128)(2,1)} %copy.102), calls=%async_computation.10 | async-start | bytes 524288 | tf_op jit(solution)/shard_map/all_to_all | solution.py:343
  611.2 214.0 %reduce-scatter.22.cloned.1.call-start = ((), (), s32[]{:S(2)}) async-start(), calls=%async_computation.23 | async-start | bytes 1310720 | tf_op jit(solution)/shard_map/reduce_scatter | solution.py:186
  616.8 3.6 copy-start.68
  616.8 5.5 copy-start.61
  616.8 5.5 copy-start.35
  616.8 5.5 copy-start.38
  620.1 278.3 %reduce-scatter.24.cloned.1.call-start = ((), (), s32[]{:S(2)}) async-start(), calls=%async_computation.24 | async-start | bytes 1622016 | tf_op jit(solution)/shard_map/reduce_scatter | solution.py:397
  626.3 198.9 %copy-start.54 = (f32[128]{0:T(128)S(1)}, f32[128]{0:T(128)}, u32[]{:S(2)}) copy-start(f32[128]{0:T(128)} %copy-done.53) | copy-start | bytes 1540
  626.3 198.9 %copy-start.59 = (f32[128]{0:T(128)S(1)}, f32[128]{0:T(128)}, u32[]{:S(2)}) copy-start(f32[128]{0:T(128)} %copy-done.58) | copy-start | bytes 1540
  626.3 200.1 %copy-start.37 = (f32[1024]{0:T(1024)S(1)}, f32[1024]{0:T(1024)}, u32[]{:S(2)}) copy-start(f32[1024]{0:T(1024)} %get-tuple-element.173) | copy-start | bytes 12292
  626.3 200.1 %copy-start.36 = (f32[1024]{0:T(1024)S(1)}, f32[1024]{0:T(1024)}, u32[]{:S(2)}) copy-start(f32[1024]{0:T(1024)} %get-tuple-element.186) | copy-start | bytes 12292
  626.3 270.1 %copy-start.16 = (f32[128,1024]{1,0:T(8,128)S(1)}, f32[128,1024]{1,0:T(8,128)}, u32[]{:S(2)}) copy-start(f32[128,1024]{1,0:T(8,128)} %copy-done.15) | copy-start | bytes 1572868
  (46 other events, 69.0 us)
Sparse Core Ops, SparseCore 0:
  133.8 20.7 all-gather.13
  156.9 45.1 all-gather.21
  282.2 20.1 reduce-scatter.15
  304.8 45.5 all-gather.23
  352.5 21.8 all-gather.15
  376.6 24.2 all-gather.17
  403.4 45.6 all-gather.25
  458.1 21.1 reduce-scatter.19
  481.7 23.0 reduce-scatter.17
  509.5 24.1 all-gather.19
  537.6 78.9 reduce-scatter.29
  620.5 78.3 reduce-scatter.27
  702.7 76.0 reduce-scatter.25
  781.2 23.3 reduce-scatter.21
  808.0 77.7 reduce-scatter.23
where the time goes:
time: 915 us; the launch traced here: 907 us
  blocking collectives  424 us (46%)
  waiting for transfers between devices  249 us (27%)
  matrix products  83.9 us (9%)
  local copies, waits for them, and re-layouts  55.9 us (6%)
  other arithmetic  41.1 us (4%)
  starting transfers between devices  36.5 us (4%)
  between operations  16.6 us (2%)
    unnamed x2, blocking collectives  189 us
    reduce_scatter x1, waiting for transfers between devices, on_device(): lax.psum_scatter(matrices[2].astype(jnp.bfloat16), ('fsdp', 'ctx'), scatt...  72.5 us
    all_gather x1, blocking collectives, on_device(): lax.all_gather(norm_bias, ('fsdp', 'ctx', 'tp'), axis=2, tiled=True)  55.9 us
    all_gather x1, blocking collectives, on_device(): lax.all_gather(out_bias, ('fsdp', 'ctx', 'tp'), axis=2, tiled=True)  53.1 us
    all_gather x1, blocking collectives, on_device(): lax.all_gather(norm_gain, ('fsdp', 'ctx', 'tp'), axis=2, tiled=True)  51.4 us
    all_gather x1, waiting for transfers between devices, fetch(): lax.all_gather(w_down[layer_index], ('fsdp', 'ctx'), axis=0, tiled=True)  48.2 us
    all_gather x1, waiting for transfers between devices, fetch(): lax.all_gather(w_qkv[layer_index], ('fsdp', 'ctx'), axis=1, tiled=True)  41.5 us
    reduce_scatter x4, waiting for transfers between devices, rows_sum(): lax.psum_scatter(partial_sum.astype(jnp.bfloat16), 'tp', scatter_dimensio...  39.2 us
  transfers between devices with their start and end apart: 23, of which 14 were waited for; matrix products, arithmetic and copies ran while one was open for 13% of the time, Pallas kernels for 0%

commit v1 on v0

v1 whole, which is shorter than its diff:
```python
import jax
import jax.numpy as jnp
from jax import lax
from jax.experimental import pallas as pl
from jax.experimental.pallas import tpu as pltpu
from jax.sharding import PartitionSpec as P

H = 16
HD = 64
EPS = 1e-05
ROOT = 0.7978845608028654
CUBIC = 0.044715
NN = (((1,), (0,)), ((), ()))
NT = (((1,), (1,)), ((), ()))
TN = (((0,), (0,)), ((), ()))
MESH = pl.DeviceIdType.MESH
F32 = jnp.float32
BF16 = jnp.bfloat16
STEPS = (1, 2, 3)

QKV = slice(0, 768)
UP = slice(768, 1792)
DOWN = slice(1792, 2816)
OUT = slice(2816, 3840)
REST = slice(768, 3840)
WIDE = 3840
SLAB = 3072
CHUNKS = 3
WIDTH = 1024
BLOCK = 256


def around(index, step):
    return lax.rem(index + step, 4)


def dot(a, b, dims=NN):
    return lax.dot_general(a, b, dims, preferred_element_type=F32)


class Copies:
    def __init__(self, send_sems, recv_sems):
        self.send_sems, self.recv_sems, self.used, self.all = send_sems, recv_sems, 0, []

    def make(self, src, dst, target):
        index = self.used
        self.used += 1
        copy = pltpu.make_async_remote_copy(
            src_ref=src,
            dst_ref=dst,
            send_sem=self.send_sems.at[index],
            recv_sem=self.recv_sems.at[index],
            device_id=target,
            device_id_type=MESH,
        )
        copy.start()
        self.all.append(copy)
        return copy

    def finish(self):
        for copy in self.all:
            copy.wait_send()


def arrived(copies):
    for copy in copies:
        copy.wait_recv()


def row_mean(x):
    return jnp.mean(x, axis=1, keepdims=True)


def layer_kernel(
    slab,
    small,
    hidden,
    cot,
    starts,
    slope_ref,
    r2_out,
    g0_out,
    slab_out,
    small_out,
    whole,
    near_c,
    near_x,
    tile_own,
    tile_z,
    pack_y,
    pack_yin,
    vec,
    bias_q,
    bias_u,
    wide1,
    gwide,
    wide2,
    gawide,
    unit1,
    unit2,
    inv1,
    inv2,
    r1,
    g1,
    qkv_out,
    qkv_in,
    q_t,
    k_t,
    v_t,
    k_n,
    v_n,
    out_t,
    lse,
    mix_t,
    mixrows_t,
    upre,
    act,
    gp16,
    part_g2,
    in_g2,
    part_dn,
    in_dn,
    part_g1,
    in_g1,
    gm_out,
    gm_in,
    gq_t,
    gk_t,
    gv_t,
    gqkv_out,
    gqkv_in,
    gqkv,
    grads,
    core_in,
    a_in,
    b_in,
    a_sum,
    b_sum,
    a_last,
    b_last,
    vsum,
    tsum,
    sz_vec,
    sz_tp,
    v1,
    t1,
    s_y,
    s_yin,
    s_g,
    sg_c,
    sg_x,
    send_sems,
    recv_sems,
    local_sems,
):
    f, k, t = lax.axis_index("fsdp"), lax.axis_index("ctx"), lax.axis_index("tp")
    z, yh = f // 2, lax.rem(f, 2)
    yl, c = k // 2, lax.rem(k, 2)
    y = yh * 2 + yl
    head = t * 4 + k
    slope = slope_ref[0, 0]

    def at_zy(zz, yy, cc):
        return (zz * 2 + yy // 2, lax.rem(yy, 2) * 2 + cc, t)

    y_peers = [at_zy(z, around(y, d), c) for d in STEPS]
    z_peers = [at_zy(around(z, d), y, c) for d in STEPS]
    sibling = at_zy(z, y, 1 - c)
    opposite = at_zy(z, around(y, 2), c)
    ctx_peers = [(f, around(k, d), t) for d in STEPS]
    tp_peers = [(f, k, around(t, d)) for d in STEPS]
    group = [(dt, dk) for dt in range(4) for dk in range(4) if (dt, dk) != (0, 0)]

    def member(dt, dk):
        return (f, around(k, dk), around(t, dt))

    barrier = pltpu.get_barrier_semaphore()
    greeted = [member(dt, dk) for dt, dk in group] + y_peers + z_peers
    for partner in greeted:
        pl.semaphore_signal(barrier, inc=1, device_id=partner, device_id_type=MESH)
    pl.semaphore_wait(barrier, len(greeted))
    copies = Copies(send_sems, recv_sems)
    make = copies.make

    small_c = [make(small, near_c.at[d - 1], ctx_peers[d - 1]) for d in STEPS]
    far = [(dt, dk) for dt, dk in group if dt]
    small_x = [
        make(small.at[pl.ds(0, 8)], near_x.at[i], member(dt, dk)) for i, (dt, dk) in enumerate(far)
    ]

    upper, lower = pl.ds(0, 16), pl.ds(16, 16)

    def spread(src, cols):
        here = whole.at[z, y, c, :, cols]
        from_y = [make(src, here, peer) for peer in y_peers]
        from_z = [make(src, here, peer) for peer in z_peers]
        return from_y, from_z

    def relay(first, cols):
        from_y, from_z = first
        block = whole.at[z, :, c, :, cols]
        via = [[] for _ in STEPS]
        for d in STEPS:
            from_y[d - 1].wait_recv()
            piece = whole.at[z, around(y, 4 - d), c, upper, cols]
            for e in STEPS:
                via[e - 1].append(make(piece, piece, z_peers[e - 1]))
            from_z[d - 1].wait_recv()
            piece = whole.at[around(z, 4 - d), y, c, lower, cols]
            for e in STEPS:
                via[d - 1].append(make(piece, piece, y_peers[e - 1]))
        return via, [make(block, block, sibling)]

    def share(state, cols):
        via, core = state
        for e in STEPS:
            arrived(via[e - 1])
            block = whole.at[around(z, 4 - e), :, c, :, cols]
            core.append(make(block, block, sibling))
        return core

    local = [
        pltpu.make_async_copy(
            slab.at[:, pl.ds(2048, 768)], whole.at[z, y, c, :, QKV], local_sems.at[0]
        ),
        pltpu.make_async_copy(
            slab.at[:, pl.ds(0, 2048)], whole.at[z, y, c, :, slice(768, 2816)], local_sems.at[1]
        ),
        pltpu.make_async_copy(
            slab.at[:, pl.ds(2816, 256)],
            whole.at[z, y, c, :, pl.ds(pl.multiple_of(2816 + t * 256, 256), 256)],
            local_sems.at[2],
        ),
    ]
    for copy in local:
        copy.start()
    qkv_first = spread(slab.at[:, pl.ds(2048, 768)], QKV)
    out_cols = whole.at[z, y, c, :, pl.ds(pl.multiple_of(2816 + t * 256, 256), 256)]
    out_x = [make(slab.at[:, pl.ds(2816, 256)], out_cols, peer) for peer in tp_peers]

    r = hidden[...].astype(F32)
    centered = r - row_mean(r)
    rstd = lax.rsqrt(row_mean(centered * centered) + EPS)
    unit1[...] = centered * rstd
    inv1[...] = rstd
    gwide[t] = cot[...].astype(BF16)

    arrived(small_c)
    arrived(small_x)
    total = small[...] + near_c[0] + near_c[1] + near_c[2]
    norms = total[0:8]
    for i in range(12):
        norms = norms + near_x[i]
    tile_own[0:8] = norms
    tile_own[8:24] = total[8:24]
    small_z = [make(tile_own, tile_z.at[d - 1], z_peers[d - 1]) for d in STEPS]
    for copy in local:
        copy.wait()
    qkv_second = relay(qkv_first, QKV)
    arrived(small_z)
    pack_y[0] = tile_own[0:8]
    columns = tile_own[8:24]
    for d in STEPS:
        pack_y[d] = tile_z[d - 1, 0:8]
        columns = columns + tile_z[d - 1, 8:24]
    pack_y[4] = columns[0:8]
    pack_y[5] = columns[8:16]
    small_y = make(pack_y, pack_yin, opposite)
    small_y.wait_recv()
    for d in range(4):
        origin = around(z, 4 - d) * 2
        vec[:, pl.ds(pl.multiple_of((origin + yh) * 128, 128), 128)] = pack_y[d]
        vec[:, pl.ds(pl.multiple_of((origin + 1 - yh) * 128, 128), 128)] = pack_yin[d]
    first_rows = pack_y[4] + pack_yin[4]
    later_rows = pack_y[5] + pack_yin[5]
    rows = [first_rows[i : i + 1] for i in range(8)] + [later_rows[i : i + 1] for i in range(6)]
    for i in range(6):
        bias_q[:, i * 128 : (i + 1) * 128] = rows[i]
    for i in range(8):
        bias_u[:, i * 128 : (i + 1) * 128] = rows[6 + i]

    wide1[t] = (unit1[...] * vec[0:1] + vec[2:3]).astype(BF16)
    wide1_x = [make(wide1.at[t], wide1.at[t], peer) for peer in tp_peers]
    qkv_core = share(qkv_second, QKV)
    arrived(out_x)
    rest_first = spread(whole.at[z, y, c, :, REST], REST)
    arrived(qkv_core)
    arrived(wide1_x)
    cot_x = [make(gwide.at[t], gwide.at[t], peer) for peer in tp_peers]

    def project(n, carry):
        cols = pl.ds(pl.multiple_of(n * 256, 256), 256)
        out = dot(wide1[...].reshape(512, 1024), whole[:, :, :, :, cols].reshape(1024, 256))
        qkv_out[cols] = (out + bias_q[:, cols]).T.astype(BF16)
        return carry

    lax.fori_loop(0, 3, project, 0)

    def head_rows(j):
        return pl.ds(pl.multiple_of(j * 192, 64), 192)

    heads_c = [
        make(qkv_out.at[head_rows(around(k, d))], qkv_in.at[k], ctx_peers[d - 1]) for d in STEPS
    ]
    qkv_in[k] = qkv_out[head_rows(k)]
    rest_second = relay(rest_first, REST)
    arrived(heads_c)
    for i in range(4):
        span = slice(i * 512, (i + 1) * 512)
        q_t[:, span] = qkv_in[i, 0:64]
        keys = qkv_in[i, 64:128]
        values = qkv_in[i, 128:192]
        k_t[:, span] = keys
        v_t[:, span] = values
        k_n[span] = keys.T
        v_n[span] = values.T

    def scores(first, begin, width):
        at = pl.ds(first, BLOCK)
        s = dot(k_n[pl.ds(begin, width)], q_t[:, at])
        key = begin + lax.broadcasted_iota(jnp.int32, (width, BLOCK), 0)
        query = first + lax.broadcasted_iota(jnp.int32, (width, BLOCK), 1)
        s = s * 0.125 + slope * (key - first).astype(F32)
        return jnp.where((key <= query) & (key >= starts[:, at]), s, -jnp.inf)

    def attend(first, begin, width):
        at = pl.ds(first, BLOCK)
        s = scores(first, begin, width)
        highest = jnp.max(s, axis=0, keepdims=True)
        e = jnp.exp(s - highest)
        totals = jnp.sum(e, axis=0, keepdims=True)
        probs = (e * (1.0 / totals)).astype(BF16)
        out_t[:, at] = dot(v_t[:, pl.ds(begin, width)], probs).astype(BF16)
        lse[:, at] = highest + jnp.log(totals)

    def blocks(body):
        for b in range(4):
            body(b * BLOCK, 0, (b + 1) * BLOCK)

        def later(b, carry):
            begin = pl.multiple_of(b * BLOCK, BLOCK)
            body(pl.multiple_of(begin + 1024, BLOCK), begin, 1024 + BLOCK)
            return carry

        lax.fori_loop(0, 4, later, 0)

    blocks(attend)

    def own_lanes(kk, tt):
        return pl.ds(pl.multiple_of(kk * 512 + tt * 128, 128), 128)

    mine_rows = pl.ds(pl.multiple_of(head * 64, 64), 64)
    mix_g = [
        make(out_t.at[:, own_lanes(around(k, dk), around(t, dt))], mix_t.at[mine_rows], member(dt, dk))
        for dt, dk in group
    ]
    mix_t[mine_rows] = out_t[:, own_lanes(k, t)]
    rest_core = share(rest_second, REST)
    arrived(mix_g)
    local_rows = pl.ds(pl.multiple_of(k * 64, 64), 64)
    mixrows_c = [
        make(
            out_t.at[:, pl.ds(pl.multiple_of(around(k, d) * 512, 512), 512)],
            mixrows_t.at[local_rows],
            ctx_peers[d - 1],
        )
        for d in STEPS
    ]
    mixrows_t[local_rows] = out_t[:, pl.ds(pl.multiple_of(k * 512, 512), 512)]
    arrived(rest_core)

    for n in range(4):
        cols = slice(n * 256, (n + 1) * 256)
        out = dot(whole[n, :, :, :, OUT].reshape(256, 1024), mix_t[...])
        r1[:, cols] = hidden[:, cols].astype(F32) + out.T + vec[4:5, cols]
    r = r1[...]
    centered = r - row_mean(r)
    rstd = lax.rsqrt(row_mean(centered * centered) + EPS)
    unit2[...] = centered * rstd
    inv2[...] = rstd
    wide2[t] = (unit2[...] * vec[1:2] + vec[3:4]).astype(BF16)
    wide2_x = [make(wide2.at[t], wide2.at[t], peer) for peer in tp_peers]
    arrived(cot_x)

    def pull(n, carry):
        cols = pl.ds(pl.multiple_of(n * 256, 256), 256)
        wcols = pl.ds(pl.multiple_of(1792 + n * 256, 256), 256)
        upre[:, cols] = dot(
            gwide[...].reshape(512, 1024), whole[:, :, :, :, wcols].reshape(1024, 256)
        )
        return carry

    lax.fori_loop(0, 4, pull, 0)
    arrived(wide2_x)

    def feed(n, carry):
        cols = pl.ds(pl.multiple_of(n * 256, 256), 256)
        wcols = pl.ds(pl.multiple_of(768 + n * 256, 256), 256)
        pre = (
            dot(wide2[...].reshape(512, 1024), whole[:, :, :, :, wcols].reshape(1024, 256))
            + bias_u[:, cols]
        )
        curve = jnp.tanh(ROOT * (pre + CUBIC * pre * pre * pre))
        act[:, cols] = (0.5 * pre * (1.0 + curve)).astype(BF16)
        slant = 0.5 * (1.0 + curve) + 0.5 * pre * (1.0 - curve * curve) * ROOT * (
            1.0 + 3.0 * CUBIC * pre * pre
        )
        gpre = upre[:, cols] * slant
        gp16[:, cols] = gpre.astype(BF16)
        bias_u[:, cols] = jnp.sum(gpre, axis=0, keepdims=True)
        return carry

    lax.fori_loop(0, 4, feed, 0)

    def partial_rows(source, cols, part):
        def one(n, carry):
            width = cols.stop - cols.start
            out = dot(source[...], whole[n, :, :, :, cols].reshape(256, width), NT)
            part[:, :, pl.ds(pl.multiple_of(n * 256, 256), 256)] = out.astype(BF16).reshape(
                4, 128, 256
            )
            return carry

        lax.fori_loop(0, 4, one, 0)

    def send_rows(part, landing):
        return [
            make(part.at[around(t, d)], landing.at[d - 1], tp_peers[d - 1]) for d in STEPS
        ]

    def sum_rows(part, landing):
        total = part[t].astype(F32)
        for d in range(3):
            total = total + landing[d].astype(F32)
        return total

    partial_rows(gp16, UP, part_g2)
    g2_x = send_rows(part_g2, in_g2)

    def matrix_grad(left, right, chunk, offset, width):
        def one(m, carry):
            rows = left[:, :, pl.ds(pl.multiple_of(m * 256, 256), 256)].reshape(512, 256)
            out = dot(rows, right[...], TN)
            grads[chunk, m, :, :, :, pl.ds(offset, width)] = out.astype(BF16).reshape(
                4, 2, 32, width
            )
            return carry

        lax.fori_loop(0, 4, one, 0)

    def reduce_core(i):
        return make(grads.at[i, :, :, 1 - c], core_in.at[i], sibling)

    def reduce_first(i, core):
        core.wait_recv()

        def add(j, carry):
            zz, yy = j // 4, lax.rem(j, 4)
            total = grads[i, zz, yy, c].astype(F32) + core_in[i, zz, yy].astype(F32)
            core_in[i, zz, yy] = total.astype(BF16)
            return carry

        lax.fori_loop(0, 16, add, 0)
        a = [
            make(core_in.at[i, around(z, d), :, upper], a_in.at[i, d - 1], z_peers[d - 1])
            for d in STEPS
        ]
        b = [
            make(core_in.at[i, :, around(y, d), lower], b_in.at[i, d - 1], y_peers[d - 1])
            for d in STEPS
        ]
        return a, b

    def reduce_second(i, state):
        a, b = state
        arrived(a)

        def add_a(j, carry):
            total = core_in[i, z, j, 0:16].astype(F32)
            for d in range(3):
                total = total + a_in[i, d, j].astype(F32)
            a_sum[i, j] = total.astype(BF16)
            return carry

        lax.fori_loop(0, 4, add_a, 0)
        a = [make(a_sum.at[i, around(y, d)], a_last.at[i, d - 1], y_peers[d - 1]) for d in STEPS]
        arrived(b)

        def add_b(j, carry):
            total = core_in[i, j, y, 16:32].astype(F32)
            for d in range(3):
                total = total + b_in[i, d, j].astype(F32)
            b_sum[i, j] = total.astype(BF16)
            return carry

        lax.fori_loop(0, 4, add_b, 0)
        b = [make(b_sum.at[i, around(z, d)], b_last.at[i, d - 1], z_peers[d - 1]) for d in STEPS]
        return a, b

    def reduce_last(i, state):
        a, b = state
        cols = slice(i * WIDTH, (i + 1) * WIDTH)
        arrived(a)
        total = a_sum[i, y].astype(F32)
        for d in range(3):
            total = total + a_last[i, d].astype(F32)
        slab_out[0:16, cols] = total
        arrived(b)
        total = b_sum[i, z].astype(F32)
        for d in range(3):
            total = total + b_last[i, d].astype(F32)
        slab_out[16:32, cols] = total

    matrix_grad(wide2, gp16, 0, 0, 1024)
    up_state = reduce_core(0)
    partial_rows(act, DOWN, part_dn)

    def norm_back(total, unit, inv, gain):
        scaled = total * gain
        return inv * (scaled - row_mean(scaled) - unit * row_mean(scaled * unit))

    arrived(g2_x)
    dn_x = send_rows(part_dn, in_dn)
    total = sum_rows(part_g2, in_g2)
    vsum[1:2] = jnp.sum(total * unit2[...], axis=0, keepdims=True)
    vsum[3:4] = jnp.sum(total, axis=0, keepdims=True)
    vsum[5:6] = jnp.sum(cot[...], axis=0, keepdims=True)
    grad_mid = cot[...] + norm_back(total, unit2[...], inv2[...], vec[1:2])
    g1[...] = grad_mid
    vsum[4:5] = jnp.sum(grad_mid, axis=0, keepdims=True)
    gawide[t] = grad_mid.astype(BF16)
    for n in range(4):
        cols = slice(n * 256, (n + 1) * 256)
        wcols = slice(2816 + n * 256, 2816 + (n + 1) * 256)
        out = dot(gawide[t], whole[:, :, :, :, wcols].reshape(1024, 256))
        gm_out[cols] = out.T.astype(BF16)
    gm_g = [
        make(
            gm_out.at[
                pl.ds(pl.multiple_of((around(t, dt) * 4 + around(k, dk)) * 64, 64), 64)
            ],
            gm_in.at[:, own_lanes(k, t)],
            member(dt, dk),
        )
        for dt, dk in group
    ]
    gm_in[:, own_lanes(k, t)] = gm_out[mine_rows]
    up_state = reduce_first(0, up_state)
    matrix_grad(gwide, act, 1, 0, 1024)
    down_state = reduce_core(1)
    arrived(gm_g)
    ga_x = [make(gawide.at[t], gawide.at[t], peer) for peer in tp_peers]
    gk_t[...] = jnp.zeros_like(gk_t)
    gv_t[...] = jnp.zeros_like(gv_t)

    def attend_back(first, begin, width):
        at = pl.ds(first, BLOCK)
        window = pl.ds(begin, width)
        p = jnp.exp(scores(first, begin, width) - lse[:, at])
        grad = gm_in[:, at]
        gv_t[:, window] += dot(grad, p.astype(BF16), NT)
        dp = dot(v_n[window], grad)
        centre = jnp.sum(p * dp, axis=0, keepdims=True)
        ds = (p * (dp - centre) * 0.125).astype(BF16)
        gq_t[:, at] = dot(k_t[:, window], ds).astype(BF16)
        gk_t[:, window] += dot(q_t[:, at], ds, NT)

    for b in range(4):
        attend_back(b * BLOCK, 0, (b + 1) * BLOCK)
    up_state = reduce_second(0, up_state)
    down_state = reduce_first(1, down_state)

    def later_back(b, carry):
        begin = pl.multiple_of(b * BLOCK, BLOCK)
        attend_back(pl.multiple_of(begin + 1024, BLOCK), begin, 1024 + BLOCK)
        return carry

    lax.fori_loop(0, 4, later_back, 0)
    for j in range(4):
        span = slice(j * 512, (j + 1) * 512)
        gqkv_out[j, 0:64] = gq_t[:, span]
        gqkv_out[j, 64:128] = gk_t[:, span].astype(BF16)
        gqkv_out[j, 128:192] = gv_t[:, span].astype(BF16)
    back_c = [
        make(gqkv_out.at[around(k, d)], gqkv_in.at[k], ctx_peers[d - 1]) for d in STEPS
    ]
    gqkv_in[k] = gqkv_out[k]
    arrived(ga_x)
    arrived(mixrows_c)
    gp16[:, 0:256] = mixrows_t[...].T
    matrix_grad(gawide, gp16.at[:, pl.ds(0, 256)], 2, 768, 256)
    reduce_last(0, up_state)
    down_state = reduce_second(1, down_state)
    arrived(dn_x)
    r2_out[...] = r1[...] + sum_rows(part_dn, in_dn) + vec[5:6]
    arrived(back_c)
    gqkv[...] = gqkv_in[...].reshape(768, 512).T
    partial_rows(gqkv, QKV, part_g1)
    g1_x = send_rows(part_g1, in_g1)
    sums = jnp.sum(gqkv[...].astype(F32), axis=0, keepdims=True)
    for i in range(6):
        tsum[i : i + 1] = sums[:, i * 128 : (i + 1) * 128]
    for i in range(8):
        tsum[6 + i : 7 + i] = bias_u[:, i * 128 : (i + 1) * 128]
    tsum[14:16] = jnp.zeros((2, 128), F32)
    matrix_grad(wide1, gqkv, 2, 0, 768)
    qkv_state = reduce_core(2)
    reduce_last(1, down_state)

    arrived(g1_x)
    qkv_state = reduce_first(2, qkv_state)
    total = sum_rows(part_g1, in_g1)
    vsum[0:1] = jnp.sum(total * unit1[...], axis=0, keepdims=True)
    vsum[2:3] = jnp.sum(total, axis=0, keepdims=True)
    vsum[6:8] = jnp.zeros((2, 1024), F32)
    sum_z = [
        make(
            vsum.at[:, pl.ds(pl.multiple_of(around(z, d) * 256, 256), 256)],
            sz_vec.at[d - 1],
            z_peers[d - 1],
        )
        for d in STEPS
    ] + [make(tsum, sz_tp.at[d - 1], z_peers[d - 1]) for d in STEPS]
    g0_out[...] = g1[...] + norm_back(total, unit1[...], inv1[...], vec[0:1])
    arrived(sum_z)
    v1[...] = (
        vsum[:, pl.ds(pl.multiple_of(z * 256, 256), 256)] + sz_vec[0] + sz_vec[1] + sz_vec[2]
    )
    t1[...] = tsum[...] + sz_tp[0] + sz_tp[1] + sz_tp[2]
    s_y[0:8] = v1[:, pl.ds(pl.multiple_of((1 - yh) * 128, 128), 128)]
    s_y[8:24] = t1[...]
    sum_y = make(s_y, s_yin, opposite)
    qkv_state = reduce_second(2, qkv_state)
    sum_y.wait_recv()
    s_g[0:8] = v1[:, pl.ds(pl.multiple_of(yh * 128, 128), 128)] + s_yin[0:8]
    s_g[8:24] = t1[...] + s_yin[8:24]
    sum_c = [make(s_g, sg_c.at[d - 1], ctx_peers[d - 1]) for d in STEPS]
    sum_x = [
        make(s_g.at[pl.ds(0, 8)], sg_x.at[i], member(dt, dk)) for i, (dt, dk) in enumerate(far)
    ]
    reduce_last(2, qkv_state)
    arrived(sum_c)
    arrived(sum_x)
    total = s_g[...] + sg_c[0] + sg_c[1] + sg_c[2]
    norms = total[0:8]
    for i in range(12):
        norms = norms + sg_x[i]
    small_out[0:8] = norms
    small_out[8:24] = total[8:24]
    copies.finish()


COUNT = 220


def run_layer(slab, small, hidden, cot, starts, slope):
    vmem = pltpu.VMEM
    scratch = [
        vmem((4, 4, 2, 32, WIDE), BF16),
        vmem((3, 24, 128), F32),
        vmem((12, 8, 128), F32),
        vmem((24, 128), F32),
        vmem((3, 24, 128), F32),
        vmem((6, 8, 128), F32),
        vmem((6, 8, 128), F32),
        vmem((8, 1024), F32),
        vmem((1, 768), F32),
        vmem((1, 1024), F32),
        vmem((4, 128, 1024), BF16),
        vmem((4, 128, 1024), BF16),
        vmem((4, 128, 1024), BF16),
        vmem((4, 128, 1024), BF16),
        vmem((128, 1024), F32),
        vmem((128, 1024), F32),
        vmem((128, 1), F32),
        vmem((128, 1), F32),
        vmem((128, 1024), F32),
        vmem((128, 1024), F32),
        vmem((768, 512), BF16),
        vmem((4, 192, 512), BF16),
        vmem((64, 2048), BF16),
        vmem((64, 2048), BF16),
        vmem((64, 2048), BF16),
        vmem((2048, 64), BF16),
        vmem((2048, 64), BF16),
        vmem((64, 2048), BF16),
        vmem((1, 2048), F32),
        vmem((1024, 128), BF16),
        vmem((256, 512), BF16),
        vmem((512, 1024), F32),
        vmem((512, 1024), BF16),
        vmem((512, 1024), BF16),
        vmem((4, 128, 1024), BF16),
        vmem((3, 128, 1024), BF16),
        vmem((4, 128, 1024), BF16),
        vmem((3, 128, 1024), BF16),
        vmem((4, 128, 1024), BF16),
        vmem((3, 128, 1024), BF16),
        vmem((1024, 128), BF16),
        vmem((64, 2048), BF16),
        vmem((64, 2048), BF16),
        vmem((64, 2048), F32),
        vmem((64, 2048), F32),
        vmem((4, 192, 512), BF16),
        vmem((4, 192, 512), BF16),
        vmem((512, 768), BF16),
        vmem((CHUNKS, 4, 4, 2, 32, WIDTH), BF16),
        vmem((CHUNKS, 4, 4, 32, WIDTH), BF16),
        vmem((CHUNKS, 3, 4, 16, WIDTH), BF16),
        vmem((CHUNKS, 3, 4, 16, WIDTH), BF16),
        vmem((CHUNKS, 4, 16, WIDTH), BF16),
        vmem((CHUNKS, 4, 16, WIDTH), BF16),
        vmem((CHUNKS, 3, 16, WIDTH), BF16),
        vmem((CHUNKS, 3, 16, WIDTH), BF16),
        vmem((8, 1024), F32),
        vmem((16, 128), F32),
        vmem((3, 8, 256), F32),
        vmem((3, 16, 128), F32),
        vmem((8, 256), F32),
        vmem((16, 128), F32),
        vmem((24, 128), F32),
        vmem((24, 128), F32),
        vmem((24, 128), F32),
        vmem((3, 24, 128), F32),
        vmem((12, 8, 128), F32),
        pltpu.SemaphoreType.DMA((COUNT,)),
        pltpu.SemaphoreType.DMA((COUNT,)),
        pltpu.SemaphoreType.DMA((3,)),
    ]
    whole_vmem = pl.BlockSpec(memory_space=pltpu.VMEM)
    return pl.pallas_call(
        layer_kernel,
        out_shape=(
            jax.ShapeDtypeStruct((128, 1024), F32),
            jax.ShapeDtypeStruct((128, 1024), F32),
            jax.ShapeDtypeStruct((32, SLAB), F32),
            jax.ShapeDtypeStruct((24, 128), F32),
        ),
        in_specs=[whole_vmem] * 5 + [pl.BlockSpec(memory_space=pltpu.SMEM)],
        out_specs=(whole_vmem,) * 4,
        scratch_shapes=scratch,
        compiler_params=pltpu.CompilerParams(
            collective_id=0, has_side_effects=True, vmem_limit_bytes=60 << 20
        ),
        name="layer",
    )(slab, small, hidden, cot, starts, slope)


def on_device(
    hidden_in,
    segment_ids,
    norm_gain,
    norm_bias,
    w_qkv,
    qv_bias,
    w_out,
    out_bias,
    w_up,
    up_bias,
    w_down,
    cotangent,
):
    f, k, t = lax.axis_index("fsdp"), lax.axis_index("ctx"), lax.axis_index("tp")
    slope = jnp.exp2(-8.0 * (t * 4 + k + 1).astype(F32) / H).reshape(1, 1)
    segments = segment_ids[0]
    starts = jnp.zeros((2048,), jnp.int32)
    for value in range(1, 4):
        starts = jnp.where(
            segments >= value, jnp.sum((segments < value).astype(jnp.int32)), starts
        )
    starts = starts.reshape(1, 2048)

    qkv_cols = w_qkv[0].reshape(3, 32, 4, 64).transpose(1, 2, 0, 3).reshape(32, 768)
    slab = jnp.concatenate([w_up[0], w_down[0], qkv_cols, w_out[0]], axis=1)

    norms = jnp.concatenate([norm_gain[0], norm_bias[0], out_bias[0], jnp.zeros((2, 8), F32)])
    lane = jnp.arange(128, dtype=jnp.int32)
    norms = jnp.where(lane[None] // 8 == k * 4 + t, jnp.tile(norms, (1, 16)), 0.0)
    qv = qv_bias[0].astype(F32)
    qv = jnp.where(lane[None, None, :64] // 2 == f * 4 + k, jnp.tile(qv, (1, 1, 32)), 0.0)
    qkv_bias = jnp.stack([qv[0], jnp.zeros_like(qv[0]), qv[1]], axis=1).reshape(6, 128)
    lane = jnp.arange(256, dtype=jnp.int32)
    up = jnp.where(
        lane[None] // 8 == f * 4 + k, jnp.tile(up_bias[0].astype(F32), (1, 32)), 0.0
    ).reshape(8, 128)
    small = jnp.concatenate([norms, qkv_bias, up, jnp.zeros((2, 128), F32)])

    hidden_out, grad_input, out, sums = run_layer(
        slab, small, hidden_in, cotangent, starts, slope
    )

    norm_sums = lax.dynamic_slice_in_dim(sums[0:6], (k * 4 + t) * 8, 8, 1)
    qkv_sums = sums[8:14].reshape(4, 3, 64)
    qv_sums = lax.dynamic_slice_in_dim(
        jnp.stack([qkv_sums[:, 0], qkv_sums[:, 2]]), (f * 4 + k) * 2, 2, 2
    )
    up_sums = lax.dynamic_slice_in_dim(sums[14:22].reshape(4, 256), (f * 4 + k) * 8, 8, 1)
    return (
        hidden_out,
        grad_input,
        norm_sums[0:2].reshape(1, 2, 8),
        norm_sums[2:4].reshape(1, 2, 8),
        out[:, 2048:2816].reshape(32, 4, 3, 64).transpose(2, 0, 1, 3).reshape(1, 3, 32, 256),
        qv_sums.reshape(1, 2, 4, 2),
        out[:, 2816:3072].reshape(1, 32, 256),
        norm_sums[4:6].reshape(1, 2, 8),
        out[:, 0:1024].reshape(1, 32, 1024),
        up_sums.reshape(1, 4, 8),
        out[:, 1024:2048].reshape(1, 32, 1024),
    )


def solution(mesh):
    return jax.shard_map(
        on_device,
        mesh=mesh,
        in_specs=(
            P(("fsdp", "ctx", "tp"), None),
            P("fsdp", None),
            P(None, None, ("fsdp", "ctx", "tp")),
            P(None, None, ("fsdp", "ctx", "tp")),
            P(None, None, ("fsdp", "ctx"), "tp"),
            P(None, None, "tp", ("fsdp", "ctx")),
            P(None, ("fsdp", "ctx"), "tp"),
            P(None, None, ("fsdp", "ctx", "tp")),
            P(None, ("fsdp", "ctx"), "tp"),
            P(None, "tp", ("fsdp", "ctx")),
            P(None, ("fsdp", "ctx"), "tp"),
            P(("fsdp", "ctx", "tp"), None),
        ),
        out_specs=(
            P(("fsdp", "ctx", "tp"), None),
            P(("fsdp", "ctx", "tp"), None),
            P(None, None, ("fsdp", "ctx", "tp")),
            P(None, None, ("fsdp", "ctx", "tp")),
            P(None, None, ("fsdp", "ctx"), "tp"),
            P(None, None, "tp", ("fsdp", "ctx")),
            P(None, ("fsdp", "ctx"), "tp"),
            P(None, None, ("fsdp", "ctx", "tp")),
            P(None, ("fsdp", "ctx"), "tp"),
            P(None, "tp", ("fsdp", "ctx")),
            P(None, ("fsdp", "ctx"), "tp"),
        ),
        check_vma=False,
    )
```

time: 915 us -> 185 us (0.20)
  blocking collectives: 424 us -> 0 us
  waiting for transfers between devices: 249 us -> 0 us
  Pallas kernels: 0 us -> 165 us
  matrix products: 83.9 us -> 0 us
  local copies, waits for them, and re-layouts: 55.9 us -> 13.2 us
  starting transfers between devices: 36.5 us -> 0 us
  other arithmetic: 41.1 us -> 4.96 us
  between operations: 16.6 us -> 0.89 us
    all_gather x6 -> x0, blocking collectives: 235 us -> none  [the longest x1 55.9 us: on_device(): lax.all_gather(norm_bias, ('fsdp', 'ctx', 'tp'), axis=2, tiled=True)]
    unnamed x2 -> x0, blocking collectives: 189 us -> none
    pallas_call x0 -> x1, Pallas kernels: none -> 165 us  [run_layer(): pl.pallas_call(layer_kernel, out_shape=(jax.ShapeDtypeStruct((128, 1024),...]
    all_gather x7 -> x0, waiting for transfers between devices: 116 us -> none  [the longest x1 48.2 us: fetch(): lax.all_gather(w_down[layer_index], ('fsdp', 'ctx'), axis=0, tiled=True)]
    reduce_scatter x7 -> x0, waiting for transfers between devices: 112 us -> none  [the longest x1 72.5 us: on_device(): lax.psum_scatter(matrices[2].astype(jnp.bfloat16), ('fsdp', 'ctx'), scatt...]
    dot_general x42 -> x0, matrix products: 83.9 us -> none  [the longest x4 12.6 us: attend_back(): jnp.einsum('qhd,khd->hqk', block_g, values_part, preferred_element_type=j...]
    all_to_all x8 -> x0, starting transfers between devices: 35.5 us -> none  [the longest x1 5.58 us: on_device(): lax.all_to_all(grad_mixed, 'ctx', split_axis=1, concat_axis=0, tiled=True)]
    slice x10 -> x4, local copies, waits for them, and re-layouts: 21.9 us -> 2.29 us  [the longest x1 0.9 us: on_device(): out[:, 2048:2816].reshape(32, 4, 3, 64).transpose(2, 0, 1, 3)]
  transfers between devices with their start and end apart: 23 -> 0, of which waited for: 14 -> 0; matrix products, arithmetic and copies ran while one was open for 13% -> 0% of each run, Pallas kernels for 0% -> 0%
where the time goes in v1:
time: 185 us; the launch traced here: 184 us
  Pallas kernels  165 us (89%)
  local copies, waits for them, and re-layouts  13.2 us (7%)
  other arithmetic  4.96 us (3%)
    pallas_call x1, Pallas kernels, run_layer(): pl.pallas_call(layer_kernel, out_shape=(jax.ShapeDtypeStruct((128, 1024),...  165 us
    unnamed x26, local copies, waits for them, and re-layouts  4.71 us

profile of v1, /device:TPU:1, one launch (start us, length us, event | category | flops | bytes accessed | tf_op | source)
XLA Modules:
  0.0 184.4 jit_solution(12077501795874759339)
XLA Ops:
  0.6 0.9 reshape_squeeze.3
  1.6 0.1 copy.52
  1.7 0.0 copy-start.3
  1.7 0.0 copy-start.4
  1.7 0.0 copy-start.6
  1.7 0.1 reshape.206
  1.8 0.7 copy-done.3
  2.5 0.0 copy-done.4
  2.5 0.7 pad_maximum_fusion.slab
  3.2 0.0 copy-start.7
  3.3 0.7 copy-done.7
  4.0 0.1 tile.32
  4.1 0.0 copy-start.8
  4.1 0.1 pad.12.clone
  4.2 0.5 copy-done.9
  4.6 0.0 copy-done.10
  4.6 0.1 copy-done.8
  4.7 0.1 maximum_maximum_fusion.1
  4.8 0.1 tile.13
  5.0 0.7 copy-done.11
  5.7 0.1 broadcast_select_fusion
  5.8 0.1 pad.7.clone
  5.9 0.1 pad_maximum_fusion.1
  5.9 0.1 copy.46
  6.0 0.1 reshape.207
  6.1 0.1 pad.5.clone
  6.2 0.7 maximum_maximum_fusion.small
  6.9 0.0 copy-done.5
  6.9 0.7 fusion
  7.6 2.6 %compare_select_fusion.2.starts = s32[1,2048]{1,0:T(1,128)} fusion(s32[1,2048]{1,0:T(1,128)S(1)} %copy-done.5, s32[]{:T(128)} %get-tuple-element.20, s32[]{:T(128)} %get-tuple-element.21, s32[]{:T(128)} %get-tuple-element.19), kind=kLoop, calls=%fused_computation.14 | loop fusion | flops 12288 | bytes 16396 | tf_op jit(solution)/shard_map/jit(_where)/select_n | solution.py:768
  10.2 165.4 %layer.1 = (f32[128,1024]{1,0:T(8,128)}, f32[128,1024]{1,0:T(8,128)}, f32[32,3072]{1,0:T(8,128)}, f32[24,128]{1,0:T(8,128)}) custom-call(bf16[32,3072]{1,0:T(8,128)(2,1)} %pad_maximum_fusion.slab, f32[24,128]{1,0:T(8,128)} %maximum_maximum_fusion.small, bf16[128,1024]{1,0:T(8,128)(2,1)} %hidden.1, f32[128,1024]{1,0:T(8,128)} %cot.1, ...), custom_call_target="tpu_custom_call" | custom-call | tf_op jit(solution)/shard_map/layer/pallas_call | solution.py:731
  175.6 0.7 fusion.6
  176.3 0.1 constant_dynamic-slice_fusion
  176.4 0.6 slice_bitcast_fusion.5
  176.9 0.9 slice.51
  177.8 0.1 reshape.211
  178.0 0.1 copy.47
  178.1 0.8 reshape.212
  178.9 0.1 reshape.213
  179.0 0.1 dynamic-slice_maximum_fusion
  179.0 0.7 copy.49
  179.7 0.6 slice_bitcast_fusion.4
  180.3 0.7 slice_bitcast_fusion
  181.0 0.7 slice.58
  181.8 0.6 dynamic-slice_bitcast_fusion
  182.4 0.8 copy.55
  183.2 0.4 copy-done
  183.6 0.8 copy.56
  (26 shorter events, 0.2 us)
Async XLA Ops:
  1.7 0.8 copy-start.3
  1.7 0.9 copy-start.4
  1.7 0.9 copy-start.6
  3.2 0.7 copy-start.7
  3.9 0.7 copy-start.9
  4.0 0.7 copy-start.10
  4.1 0.7 copy-start.8
  5.0 0.7 copy-start.11
  6.2 0.7 copy-start.5
  178.0 1.7 copy-start.2
  178.1 4.4 %copy-start.1 = (f32[128,1024]{1,0:T(8,128)S(1)}, f32[128,1024]{1,0:T(8,128)}, u32[]{:S(2)}) copy-start(f32[128,1024]{1,0:T(8,128)} %get-tuple-element.46) | copy-start | bytes 1572868
  182.4 1.2 copy-start

commit v2 on v1

--- a/solution.py
+++ b/solution.py
@@ -22,11 +22,10 @@
 UP = slice(768, 1792)
 DOWN = slice(1792, 2816)
 OUT = slice(2816, 3840)
-REST = slice(768, 3840)
+MLP = slice(768, 2816)
 WIDE = 3840
 SLAB = 3072
-CHUNKS = 3
-WIDTH = 1024
+CHUNKS = ((0, 1024), (1024, 1024), (2816, 256), (2048, 768))
 BLOCK = 256
 
 
@@ -45,6 +44,7 @@
     def make(self, src, dst, target):
         index = self.used
         self.used += 1
+        assert index < COUNT
         copy = pltpu.make_async_remote_copy(
             src_ref=src,
             dst_ref=dst,
@@ -62,6 +62,11 @@
             copy.wait_send()
 
 
+def step(*works):
+    for work in works:
+        next(work, None)
+
+
 def arrived(copies):
     for copy in copies:
         copy.wait_recv()
@@ -72,17 +77,25 @@
 
 
 def layer_kernel(
-    slab,
-    small,
+    w_up,
+    w_down,
+    w_qkv,
+    w_out,
+    gain_in,
+    shift_in,
+    obias_in,
+    qv_in,
+    ub_in,
     hidden,
     cot,
-    starts,
-    slope_ref,
+    segments,
     r2_out,
     g0_out,
     slab_out,
     small_out,
     whole,
+    small,
+    starts,
     near_c,
     near_x,
     tile_own,
@@ -117,10 +130,13 @@
     act,
     gp16,
     part_g2,
+    via_g2,
     in_g2,
     part_dn,
+    via_dn,
     in_dn,
     part_g1,
+    via_g1,
     in_g1,
     gm_out,
     gm_in,
@@ -132,10 +148,14 @@
     gqkv,
     grads,
     core_in,
+    a_via,
+    b_via,
     a_in,
     b_in,
     a_sum,
     b_sum,
+    a_lastvia,
+    b_lastvia,
     a_last,
     b_last,
     vsum,
@@ -151,14 +171,14 @@
     sg_x,
     send_sems,
     recv_sems,
-    local_sems,
 ):
     f, k, t = lax.axis_index("fsdp"), lax.axis_index("ctx"), lax.axis_index("tp")
     z, yh = f // 2, lax.rem(f, 2)
     yl, c = k // 2, lax.rem(k, 2)
     y = yh * 2 + yl
     head = t * 4 + k
-    slope = slope_ref[0, 0]
+    place = f * 4 + k
+    slope = jnp.exp2(jnp.full((1, BLOCK), -8.0 / H, F32) * (head + 1).astype(F32))
 
     def at_zy(zz, yy, cc):
         return (zz * 2 + yy // 2, lax.rem(yy, 2) * 2 + cc, t)
@@ -182,6 +202,37 @@
     copies = Copies(send_sems, recv_sems)
     make = copies.make
 
+    def lanes(count, period, index):
+        row = lax.broadcasted_iota(jnp.int32, (count, 128), 0)
+        lane = lax.broadcasted_iota(jnp.int32, (count, 128), 1)
+        return ((lane % count == row) & ((lane % period) // count == index)).astype(F32)
+
+    def scatter(values, hot):
+        return lax.dot_general(
+            values.astype(F32), hot, NN, precision=lax.Precision.HIGHEST, preferred_element_type=F32
+        )
+
+    small[...] = jnp.zeros_like(small)
+    own = lanes(8, 128, k * 4 + t)
+    small[0:2] = scatter(gain_in[0], own)
+    small[2:4] = scatter(shift_in[0], own)
+    small[4:6] = scatter(obias_in[0], own)
+    pair = lanes(2, 64, place)
+    left = lax.broadcasted_iota(jnp.int32, (4, 128), 1) < 64
+    q_row, v_row = scatter(qv_in[0, 0], pair), scatter(qv_in[0, 1], pair)
+    q_left, q_right = jnp.where(left, q_row, 0.0), jnp.where(left, 0.0, q_row)
+    v_left, v_right = jnp.where(left, v_row, 0.0), jnp.where(left, 0.0, v_row)
+    small[8:9] = q_left[0:1]
+    small[9:10] = v_left[0:1] + q_right[1:2]
+    small[10:11] = v_right[1:2]
+    small[11:12] = q_left[2:3]
+    small[12:13] = v_left[2:3] + q_right[3:4]
+    small[13:14] = v_right[3:4]
+    up_row = scatter(ub_in[0], lanes(8, 128, lax.rem(place, 16)))
+    even = (place < 16).astype(F32)
+    for i in range(4):
+        small[14 + 2 * i : 15 + 2 * i] = up_row[i : i + 1] * even
+        small[15 + 2 * i : 16 + 2 * i] = up_row[i : i + 1] * (1.0 - even)
     small_c = [make(small, near_c.at[d - 1], ctx_peers[d - 1]) for d in STEPS]
     far = [(dt, dk) for dt, dk in group if dt]
     small_x = [
@@ -189,61 +240,112 @@
     ]
 
     upper, lower = pl.ds(0, 16), pl.ds(16, 16)
-
-    def spread(src, cols):
-        here = whole.at[z, y, c, :, cols]
-        from_y = [make(src, here, peer) for peer in y_peers]
-        from_z = [make(src, here, peer) for peer in z_peers]
-        return from_y, from_z
-
-    def relay(first, cols):
-        from_y, from_z = first
-        block = whole.at[z, :, c, :, cols]
-        via = [[] for _ in STEPS]
+    low, high = pl.ds(0, 2), pl.ds(2, 2)
+
+    def ring(part, me, peers):
+        plus, minus = peers[0], peers[2]
+        u, v = part(me)
+        plus_u, minus_v = make(u, u, plus), make(v, v, minus)
+        plus_v, minus_u = make(v, v, plus), make(u, u, minus)
+
+        def forward():
+            plus_u.wait_recv()
+            u = part(around(me, 3))[0]
+            next_u = make(u, u, plus)
+            minus_v.wait_recv()
+            v = part(around(me, 1))[1]
+            return [plus_v, minus_u, next_u, make(v, v, minus)]
+
+        return forward
+
+    def ring_rows(buffer):
+        return ring(
+            lambda o: (buffer.at[o, :, pl.ds(0, 512)], buffer.at[o, :, pl.ds(512, 512)]),
+            t,
+            tp_peers,
+        )
+
+    def ring_sum(part, via, land, me, peers, filled=None):
+        plus, minus = peers[0], peers[2]
+        one, two, three = around(me, 1), around(me, 2), around(me, 3)
+        if filled:
+            filled(0)
+        via_u = make(part(two)[0], via[0], plus)
+        near_u = make(part(three)[0], land[1][0], minus)
+        if filled:
+            filled(1)
+        via_v = make(part(two)[1], via[1], minus)
+        near_v = make(part(one)[1], land[0][1], plus)
+        yield
+        via_u.wait_recv()
+        via[0][...] = (via[0][...].astype(F32) + part(one)[0][...].astype(F32)).astype(BF16)
+        next_u = make(via[0], land[0][0], plus)
+        via_v.wait_recv()
+        via[1][...] = (via[1][...].astype(F32) + part(three)[1][...].astype(F32)).astype(BF16)
+        next_v = make(via[1], land[1][1], minus)
+        yield
+        arrived([near_u, near_v, next_u, next_v])
+
+    def ring_sum_rows(part, via, land, filled=None):
+        ends = pl.ds(0, 512), pl.ds(512, 512)
+        return ring_sum(
+            lambda o: tuple(part.at[o, :, end] for end in ends),
+            (via.at[0], via.at[1]),
+            tuple(tuple(land.at[i, :, end] for end in ends) for i in range(2)),
+            t,
+            tp_peers,
+            filled,
+        )
+
+    def gather(cols):
+        middle = (cols.start + cols.stop) // 2
+        ends = slice(cols.start, middle), slice(middle, cols.stop)
+        a = ring(lambda o: tuple(whole.at[z, o, c, upper, end] for end in ends), y, y_peers)
+        b = ring(lambda o: tuple(whole.at[o, y, c, lower, end] for end in ends), z, z_peers)
+        yield
+        a, b = a(), b()
+        yield
+        arrived(a)
+        a = ring(lambda o: tuple(whole.at[o, yy, c, upper, cols] for yy in (low, high)), z, z_peers)
+        arrived(b)
+        b = ring(lambda o: tuple(whole.at[zz, o, c, lower, cols] for zz in (low, high)), y, y_peers)
+
+        def both(d):
+            for block in (
+                whole.at[around(z, d), :, c, upper, cols],
+                whole.at[:, around(y, d), c, lower, cols],
+            ):
+                core.append(make(block, block, sibling))
+
+        core = []
+        both(0)
+        yield
+        a, b = a(), b()
+        yield
+        arrived(a + b)
         for d in STEPS:
-            from_y[d - 1].wait_recv()
-            piece = whole.at[z, around(y, 4 - d), c, upper, cols]
-            for e in STEPS:
-                via[e - 1].append(make(piece, piece, z_peers[e - 1]))
-            from_z[d - 1].wait_recv()
-            piece = whole.at[around(z, 4 - d), y, c, lower, cols]
-            for e in STEPS:
-                via[d - 1].append(make(piece, piece, y_peers[e - 1]))
-        return via, [make(block, block, sibling)]
-
-    def share(state, cols):
-        via, core = state
-        for e in STEPS:
-            arrived(via[e - 1])
-            block = whole.at[around(z, 4 - e), :, c, :, cols]
-            core.append(make(block, block, sibling))
-        return core
-
-    local = [
-        pltpu.make_async_copy(
-            slab.at[:, pl.ds(2048, 768)], whole.at[z, y, c, :, QKV], local_sems.at[0]
-        ),
-        pltpu.make_async_copy(
-            slab.at[:, pl.ds(0, 2048)], whole.at[z, y, c, :, slice(768, 2816)], local_sems.at[1]
-        ),
-        pltpu.make_async_copy(
-            slab.at[:, pl.ds(2816, 256)],
-            whole.at[z, y, c, :, pl.ds(pl.multiple_of(2816 + t * 256, 256), 256)],
-            local_sems.at[2],
-        ),
-    ]
-    for copy in local:
-        copy.start()
-    qkv_first = spread(slab.at[:, pl.ds(2048, 768)], QKV)
-    out_cols = whole.at[z, y, c, :, pl.ds(pl.multiple_of(2816 + t * 256, 256), 256)]
-    out_x = [make(slab.at[:, pl.ds(2816, 256)], out_cols, peer) for peer in tp_peers]
+            both(d)
+        yield
+        arrived(core)
+
+    for j in range(4):
+        for i in range(3):
+            col = j * 192 + i * 64
+            whole[z, y, c, :, col : col + 64] = w_qkv[0, i, :, j * 64 : j * 64 + 64]
+    gather_qkv = gather(QKV)
+    step(gather_qkv)
+    own_out = pl.ds(pl.multiple_of(2816 + t * 256, 256), 256)
+    whole[z, y, c, :, own_out] = w_out[0]
+    out_cols = whole.at[z, y, c, :, own_out]
+    out_x = [make(out_cols, out_cols, peer) for peer in tp_peers]
+    whole[z, y, c, :, 768:1792] = w_up[0]
+    whole[z, y, c, :, 1792:2816] = w_down[0]
 
     r = hidden[...].astype(F32)
     centered = r - row_mean(r)
     rstd = lax.rsqrt(row_mean(centered * centered) + EPS)
     unit1[...] = centered * rstd
     inv1[...] = rstd
-    gwide[t] = cot[...].astype(BF16)
 
     arrived(small_c)
     arrived(small_x)
@@ -254,9 +356,7 @@
     tile_own[0:8] = norms
     tile_own[8:24] = total[8:24]
     small_z = [make(tile_own, tile_z.at[d - 1], z_peers[d - 1]) for d in STEPS]
-    for copy in local:
-        copy.wait()
-    qkv_second = relay(qkv_first, QKV)
+    step(gather_qkv)
     arrived(small_z)
     pack_y[0] = tile_own[0:8]
     columns = tile_own[8:24]
@@ -266,6 +366,7 @@
     pack_y[4] = columns[0:8]
     pack_y[5] = columns[8:16]
     small_y = make(pack_y, pack_yin, opposite)
+    step(gather_qkv)
     small_y.wait_recv()
     for d in range(4):
         origin = around(z, 4 - d) * 2
@@ -280,13 +381,24 @@
         bias_u[:, i * 128 : (i + 1) * 128] = rows[6 + i]
 
     wide1[t] = (unit1[...] * vec[0:1] + vec[2:3]).astype(BF16)
-    wide1_x = [make(wide1.at[t], wide1.at[t], peer) for peer in tp_peers]
-    qkv_core = share(qkv_second, QKV)
+    wide1_x = ring_rows(wide1)
+    step(gather_qkv)
     arrived(out_x)
-    rest_first = spread(whole.at[z, y, c, :, REST], REST)
-    arrived(qkv_core)
+    gather_out = gather(OUT)
+    step(gather_out)
+    wide1_x = wide1_x()
+    gwide[t] = cot[...].astype(BF16)
+    ids = segments[...]
+    first = jnp.zeros((1, 2048), F32)
+    for value in range(1, 4):
+        count = jnp.sum((ids < value).astype(F32), axis=1, keepdims=True)
+        first = jnp.where(ids >= value, count, first)
+    starts[...] = first
+    step(gather_qkv)
+    step(gather_out)
+    step(gather_qkv)
     arrived(wide1_x)
-    cot_x = [make(gwide.at[t], gwide.at[t], peer) for peer in tp_peers]
+    gwide_x = ring_rows(gwide)
 
     def project(n, carry):
         cols = pl.ds(pl.multiple_of(n * 256, 256), 256)
@@ -303,7 +415,11 @@
         make(qkv_out.at[head_rows(around(k, d))], qkv_in.at[k], ctx_peers[d - 1]) for d in STEPS
     ]
     qkv_in[k] = qkv_out[head_rows(k)]
-    rest_second = relay(rest_first, REST)
+    step(gather_out)
+    gather_mlp = gather(MLP)
+    step(gather_mlp)
+    gwide_x = gwide_x()
+    step(gather_out)
     arrived(heads_c)
     for i in range(4):
         span = slice(i * 512, (i + 1) * 512)
@@ -321,7 +437,7 @@
         key = begin + lax.broadcasted_iota(jnp.int32, (width, BLOCK), 0)
         query = first + lax.broadcasted_iota(jnp.int32, (width, BLOCK), 1)
         s = s * 0.125 + slope * (key - first).astype(F32)
-        return jnp.where((key <= query) & (key >= starts[:, at]), s, -jnp.inf)
+        return jnp.where((key <= query) & (key.astype(F32) >= starts[:, at]), s, -jnp.inf)
 
     def attend(first, begin, width):
         at = pl.ds(first, BLOCK)
@@ -333,18 +449,29 @@
         out_t[:, at] = dot(v_t[:, pl.ds(begin, width)], probs).astype(BF16)
         lse[:, at] = highest + jnp.log(totals)
 
-    def blocks(body):
-        for b in range(4):
-            body(b * BLOCK, 0, (b + 1) * BLOCK)
-
+    def blocks(body, *between):
         def later(b, carry):
             begin = pl.multiple_of(b * BLOCK, BLOCK)
             body(pl.multiple_of(begin + 1024, BLOCK), begin, 1024 + BLOCK)
             return carry
 
-        lax.fori_loop(0, 4, later, 0)
-
-    blocks(attend)
+        for b in range(4):
+            body(b * BLOCK, 0, (b + 1) * BLOCK)
+            if b == 1:
+                between[0]()
+        between[1]()
+        lax.fori_loop(0, 2, later, 0)
+        between[2]()
+        lax.fori_loop(2, 4, later, 0)
+        between[3]()
+
+    blocks(
+        attend,
+        lambda: step(gather_out, gather_mlp),
+        lambda: step(gather_mlp),
+        lambda: step(gather_mlp),
+        lambda: None,
+    )
 
     def own_lanes(kk, tt):
         return pl.ds(pl.multiple_of(kk * 512 + tt * 128, 128), 128)
@@ -355,7 +482,7 @@
         for dt, dk in group
     ]
     mix_t[mine_rows] = out_t[:, own_lanes(k, t)]
-    rest_core = share(rest_second, REST)
+    step(gather_out, gather_mlp)
     arrived(mix_g)
     local_rows = pl.ds(pl.multiple_of(k * 64, 64), 64)
     mixrows_c = [
@@ -367,7 +494,6 @@
         for d in STEPS
     ]
     mixrows_t[local_rows] = out_t[:, pl.ds(pl.multiple_of(k * 512, 512), 512)]
-    arrived(rest_core)
 
     for n in range(4):
         cols = slice(n * 256, (n + 1) * 256)
@@ -379,8 +505,9 @@
     unit2[...] = centered * rstd
     inv2[...] = rstd
     wide2[t] = (unit2[...] * vec[1:2] + vec[3:4]).astype(BF16)
-    wide2_x = [make(wide2.at[t], wide2.at[t], peer) for peer in tp_peers]
-    arrived(cot_x)
+    wide2_x = ring_rows(wide2)
+    step(gather_mlp)
+    arrived(gwide_x)
 
     def pull(n, carry):
         cols = pl.ds(pl.multiple_of(n * 256, 256), 256)
@@ -390,7 +517,9 @@
         )
         return carry
 
-    lax.fori_loop(0, 4, pull, 0)
+    lax.fori_loop(0, 2, pull, 0)
+    wide2_x = wide2_x()
+    lax.fori_loop(2, 4, pull, 0)
     arrived(wide2_x)
 
     def feed(n, carry):
@@ -421,106 +550,114 @@
             )
             return carry
 
-        lax.fori_loop(0, 4, one, 0)
-
-    def send_rows(part, landing):
-        return [
-            make(part.at[around(t, d)], landing.at[d - 1], tp_peers[d - 1]) for d in STEPS
-        ]
+        return lambda half: lax.fori_loop(2 * half, 2 * half + 2, one, 0)
 
     def sum_rows(part, landing):
-        total = part[t].astype(F32)
-        for d in range(3):
-            total = total + landing[d].astype(F32)
-        return total
-
-    partial_rows(gp16, UP, part_g2)
-    g2_x = send_rows(part_g2, in_g2)
-
-    def matrix_grad(left, right, chunk, offset, width):
+        return part[t].astype(F32) + landing[0].astype(F32) + landing[1].astype(F32)
+
+    sum_g2 = ring_sum_rows(part_g2, via_g2, in_g2, partial_rows(gp16, UP, part_g2))
+    step(sum_g2)
+
+    def matrix_grad(left, right, chunk):
+        width = CHUNKS[chunk][1]
+
         def one(m, carry):
             rows = left[:, :, pl.ds(pl.multiple_of(m * 256, 256), 256)].reshape(512, 256)
             out = dot(rows, right[...], TN)
-            grads[chunk, m, :, :, :, pl.ds(offset, width)] = out.astype(BF16).reshape(
-                4, 2, 32, width
-            )
+            grads[chunk][m] = out.astype(BF16).reshape(4, 2, 32, width)
             return carry
 
         lax.fori_loop(0, 4, one, 0)
 
-    def reduce_core(i):
-        return make(grads.at[i, :, :, 1 - c], core_in.at[i], sibling)
-
-    def reduce_first(i, core):
+    def reduce(i):
+        offset, width = CHUNKS[i]
+        both = core_in[i]
+        core = make(grads[i].at[:, :, 1 - c], both, sibling)
+        yield
         core.wait_recv()
 
         def add(j, carry):
             zz, yy = j // 4, lax.rem(j, 4)
-            total = grads[i, zz, yy, c].astype(F32) + core_in[i, zz, yy].astype(F32)
-            core_in[i, zz, yy] = total.astype(BF16)
+            total = grads[i][zz, yy, c].astype(F32) + both[zz, yy].astype(F32)
+            both[zz, yy] = total.astype(BF16)
             return carry
 
         lax.fori_loop(0, 16, add, 0)
-        a = [
-            make(core_in.at[i, around(z, d), :, upper], a_in.at[i, d - 1], z_peers[d - 1])
-            for d in STEPS
-        ]
-        b = [
-            make(core_in.at[i, :, around(y, d), lower], b_in.at[i, d - 1], y_peers[d - 1])
-            for d in STEPS
-        ]
-        return a, b
-
-    def reduce_second(i, state):
-        a, b = state
-        arrived(a)
-
-        def add_a(j, carry):
-            total = core_in[i, z, j, 0:16].astype(F32)
-            for d in range(3):
-                total = total + a_in[i, d, j].astype(F32)
-            a_sum[i, j] = total.astype(BF16)
-            return carry
-
-        lax.fori_loop(0, 4, add_a, 0)
-        a = [make(a_sum.at[i, around(y, d)], a_last.at[i, d - 1], y_peers[d - 1]) for d in STEPS]
-        arrived(b)
-
-        def add_b(j, carry):
-            total = core_in[i, j, y, 16:32].astype(F32)
-            for d in range(3):
-                total = total + b_in[i, d, j].astype(F32)
-            b_sum[i, j] = total.astype(BF16)
-            return carry
-
-        lax.fori_loop(0, 4, add_b, 0)
-        b = [make(b_sum.at[i, around(z, d)], b_last.at[i, d - 1], z_peers[d - 1]) for d in STEPS]
-        return a, b
-
-    def reduce_last(i, state):
-        a, b = state
-        cols = slice(i * WIDTH, (i + 1) * WIDTH)
-        arrived(a)
-        total = a_sum[i, y].astype(F32)
-        for d in range(3):
-            total = total + a_last[i, d].astype(F32)
-        slab_out[0:16, cols] = total
-        arrived(b)
-        total = b_sum[i, z].astype(F32)
-        for d in range(3):
-            total = total + b_last[i, d].astype(F32)
-        slab_out[16:32, cols] = total
-
-    matrix_grad(wide2, gp16, 0, 0, 1024)
-    up_state = reduce_core(0)
-    partial_rows(act, DOWN, part_dn)
+        yield
+        a = ring_sum(
+            lambda o: (both.at[o, low, upper], both.at[o, high, upper]),
+            (a_via[i].at[low], a_via[i].at[high]),
+            tuple((a_in[i].at[d, low], a_in[i].at[d, high]) for d in range(2)),
+            z,
+            z_peers,
+        )
+        b = ring_sum(
+            lambda o: (both.at[low, o, lower], both.at[high, o, lower]),
+            (b_via[i].at[low], b_via[i].at[high]),
+            tuple((b_in[i].at[d, low], b_in[i].at[d, high]) for d in range(2)),
+            y,
+            y_peers,
+        )
+        step(a, b)
+        yield
+        step(a, b)
+        yield
+        step(a)
+        for j in range(4):
+            total = both[z, j, 0:16].astype(F32)
+            for d in range(2):
+                total = total + a_in[i][d, j].astype(F32)
+            a_sum[i][j] = total.astype(BF16)
+        ends = pl.ds(0, width // 2), pl.ds(width // 2, width // 2)
+        a = ring_sum(
+            lambda o: tuple(a_sum[i].at[o, :, end] for end in ends),
+            tuple(a_lastvia[i].at[:, end] for end in ends),
+            tuple(tuple(a_last[i].at[d, :, end] for end in ends) for d in range(2)),
+            y,
+            y_peers,
+        )
+        step(a)
+        step(b)
+        for j in range(4):
+            total = both[j, y, 16:32].astype(F32)
+            for d in range(2):
+                total = total + b_in[i][d, j].astype(F32)
+            b_sum[i][j] = total.astype(BF16)
+        b = ring_sum(
+            lambda o: tuple(b_sum[i].at[o, :, end] for end in ends),
+            tuple(b_lastvia[i].at[:, end] for end in ends),
+            tuple(tuple(b_last[i].at[d, :, end] for end in ends) for d in range(2)),
+            z,
+            z_peers,
+        )
+        step(b)
+        yield
+        step(a, b)
+        yield
+        step(a, b)
+        cols = slice(offset, offset + width)
+        slab_out[0:16, cols] = (
+            a_sum[i][y].astype(F32) + a_last[i][0].astype(F32) + a_last[i][1].astype(F32)
+        )
+        slab_out[16:32, cols] = (
+            b_sum[i][z].astype(F32) + b_last[i][0].astype(F32) + b_last[i][1].astype(F32)
+        )
+
+    matrix_grad(wide2, gp16, 0)
+    reduce_up = reduce(0)
+    step(reduce_up, sum_g2)
+    down_rows = partial_rows(act, DOWN, part_dn)
+    down_rows(0)
+    down_rows(1)
+    matrix_grad(gwide, act, 1)
+    reduce_down = reduce(1)
+    step(reduce_down)
 
     def norm_back(total, unit, inv, gain):
         scaled = total * gain
         return inv * (scaled - row_mean(scaled) - unit * row_mean(scaled * unit))
 
-    arrived(g2_x)
-    dn_x = send_rows(part_dn, in_dn)
+    step(sum_g2)
     total = sum_rows(part_g2, in_g2)
     vsum[1:2] = jnp.sum(total * unit2[...], axis=0, keepdims=True)
     vsum[3:4] = jnp.sum(total, axis=0, keepdims=True)
@@ -545,11 +682,10 @@
         for dt, dk in group
     ]
     gm_in[:, own_lanes(k, t)] = gm_out[mine_rows]
-    up_state = reduce_first(0, up_state)
-    matrix_grad(gwide, act, 1, 0, 1024)
-    down_state = reduce_core(1)
+    step(reduce_up, reduce_down)
     arrived(gm_g)
-    ga_x = [make(gawide.at[t], gawide.at[t], peer) for peer in tp_peers]
+    gawide_x = ring_rows(gawide)
+    step(reduce_up)
     gk_t[...] = jnp.zeros_like(gk_t)
     gv_t[...] = jnp.zeros_like(gv_t)
 
@@ -565,17 +701,22 @@
         gq_t[:, at] = dot(k_t[:, window], ds).astype(BF16)
         gk_t[:, window] += dot(q_t[:, at], ds, NT)
 
-    for b in range(4):
-        attend_back(b * BLOCK, 0, (b + 1) * BLOCK)
-    up_state = reduce_second(0, up_state)
-    down_state = reduce_first(1, down_state)
-
-    def later_back(b, carry):
-        begin = pl.multiple_of(b * BLOCK, BLOCK)
-        attend_back(pl.multiple_of(begin + 1024, BLOCK), begin, 1024 + BLOCK)
-        return carry
-
-    lax.fori_loop(0, 4, later_back, 0)
+    sum_dn = ring_sum_rows(part_dn, via_dn, in_dn)
+    waiting = []
+
+    def second():
+        step(reduce_up, reduce_down)
+        waiting.append(gawide_x())
+        step(sum_dn)
+
+    blocks(
+        attend_back,
+        second,
+        lambda: step(reduce_up, reduce_down, sum_dn),
+        lambda: step(reduce_up, reduce_down, sum_dn),
+        lambda: None,
+    )
+    gawide_x = waiting[0]
     for j in range(4):
         span = slice(j * 512, (j + 1) * 512)
         gqkv_out[j, 0:64] = gq_t[:, span]
@@ -585,30 +726,31 @@
         make(gqkv_out.at[around(k, d)], gqkv_in.at[k], ctx_peers[d - 1]) for d in STEPS
     ]
     gqkv_in[k] = gqkv_out[k]
-    arrived(ga_x)
+    arrived(gawide_x)
     arrived(mixrows_c)
     gp16[:, 0:256] = mixrows_t[...].T
-    matrix_grad(gawide, gp16.at[:, pl.ds(0, 256)], 2, 768, 256)
-    reduce_last(0, up_state)
-    down_state = reduce_second(1, down_state)
-    arrived(dn_x)
+    matrix_grad(gawide, gp16.at[:, pl.ds(0, 256)], 2)
+    reduce_out = reduce(2)
+    step(reduce_out, reduce_up, reduce_down)
     r2_out[...] = r1[...] + sum_rows(part_dn, in_dn) + vec[5:6]
     arrived(back_c)
     gqkv[...] = gqkv_in[...].reshape(768, 512).T
-    partial_rows(gqkv, QKV, part_g1)
-    g1_x = send_rows(part_g1, in_g1)
+    sum_g1 = ring_sum_rows(part_g1, via_g1, in_g1, partial_rows(gqkv, QKV, part_g1))
+    step(sum_g1)
+    step(reduce_out, reduce_down)
     sums = jnp.sum(gqkv[...].astype(F32), axis=0, keepdims=True)
     for i in range(6):
         tsum[i : i + 1] = sums[:, i * 128 : (i + 1) * 128]
     for i in range(8):
         tsum[6 + i : 7 + i] = bias_u[:, i * 128 : (i + 1) * 128]
     tsum[14:16] = jnp.zeros((2, 128), F32)
-    matrix_grad(wide1, gqkv, 2, 0, 768)
-    qkv_state = reduce_core(2)
-    reduce_last(1, down_state)
-
-    arrived(g1_x)
-    qkv_state = reduce_first(2, qkv_state)
+    matrix_grad(wide1, gqkv, 3)
+    reduce_qkv = reduce(3)
+    step(reduce_qkv, sum_g1, reduce_out)
+
+    step(reduce_qkv)
+    step(reduce_qkv)
+    step(sum_g1)
     total = sum_rows(part_g1, in_g1)
     vsum[0:1] = jnp.sum(total * unit1[...], axis=0, keepdims=True)
     vsum[2:3] = jnp.sum(total, axis=0, keepdims=True)
@@ -621,6 +763,7 @@
         )
         for d in STEPS
     ] + [make(tsum, sz_tp.at[d - 1], z_peers[d - 1]) for d in STEPS]
+    step(reduce_qkv, reduce_out)
     g0_out[...] = g1[...] + norm_back(total, unit1[...], inv1[...], vec[0:1])
     arrived(sum_z)
     v1[...] = (
@@ -630,7 +773,7 @@
     s_y[0:8] = v1[:, pl.ds(pl.multiple_of((1 - yh) * 128, 128), 128)]
     s_y[8:24] = t1[...]
     sum_y = make(s_y, s_yin, opposite)
-    qkv_state = reduce_second(2, qkv_state)
+    step(reduce_qkv, reduce_out)
     sum_y.wait_recv()
     s_g[0:8] = v1[:, pl.ds(pl.multiple_of(yh * 128, 128), 128)] + s_yin[0:8]
     s_g[8:24] = t1[...] + s_yin[8:24]
@@ -638,7 +781,9 @@
     sum_x = [
         make(s_g.at[pl.ds(0, 8)], sg_x.at[i], member(dt, dk)) for i, (dt, dk) in enumerate(far)
     ]
-    reduce_last(2, qkv_state)
+    step(reduce_qkv, reduce_out)
+    step(reduce_qkv, reduce_out)
+    step(reduce_up, reduce_down)
     arrived(sum_c)
     arrived(sum_x)
     total = s_g[...] + sg_c[0] + sg_c[1] + sg_c[2]
@@ -650,13 +795,19 @@
     copies.finish()
 
 
-COUNT = 220
-
-
-def run_layer(slab, small, hidden, cot, starts, slope):
+COUNT = 336
+
+
+def run_layer(*operands):
     vmem = pltpu.VMEM
+
+    def per_chunk(*shape):
+        return tuple(vmem((*shape, width), BF16) for _, width in CHUNKS)
+
     scratch = [
         vmem((4, 4, 2, 32, WIDE), BF16),
+        vmem((24, 128), F32),
+        vmem((1, 2048), F32),
         vmem((3, 24, 128), F32),
         vmem((12, 8, 128), F32),
         vmem((24, 128), F32),
@@ -691,11 +842,14 @@
         vmem((512, 1024), BF16),
         vmem((512, 1024), BF16),
         vmem((4, 128, 1024), BF16),
-        vmem((3, 128, 1024), BF16),
+        vmem((2, 128, 512), BF16),
+        vmem((2, 128, 1024), BF16),
         vmem((4, 128, 1024), BF16),
-        vmem((3, 128, 1024), BF16),
+        vmem((2, 128, 512), BF16),
+        vmem((2, 128, 1024), BF16),
         vmem((4, 128, 1024), BF16),
-        vmem((3, 128, 1024), BF16),
+        vmem((2, 128, 512), BF16),
+        vmem((2, 128, 1024), BF16),
         vmem((1024, 128), BF16),
         vmem((64, 2048), BF16),
         vmem((64, 2048), BF16),
@@ -704,14 +858,18 @@
         vmem((4, 192, 512), BF16),
         vmem((4, 192, 512), BF16),
         vmem((512, 768), BF16),
-        vmem((CHUNKS, 4, 4, 2, 32, WIDTH), BF16),
-        vmem((CHUNKS, 4, 4, 32, WIDTH), BF16),
-        vmem((CHUNKS, 3, 4, 16, WIDTH), BF16),
-        vmem((CHUNKS, 3, 4, 16, WIDTH), BF16),
-        vmem((CHUNKS, 4, 16, WIDTH), BF16),
-        vmem((CHUNKS, 4, 16, WIDTH), BF16),
-        vmem((CHUNKS, 3, 16, WIDTH), BF16),
-        vmem((CHUNKS, 3, 16, WIDTH), BF16),
+        per_chunk(4, 4, 2, 32),
+        per_chunk(4, 4, 32),
+        per_chunk(4, 16),
+        per_chunk(4, 16),
+        per_chunk(2, 4, 16),
+        per_chunk(2, 4, 16),
+        per_chunk(4, 16),
+        per_chunk(4, 16),
+        per_chunk(16),
+        per_chunk(16),
+        per_chunk(2, 16),
+        per_chunk(2, 16),
         vmem((8, 1024), F32),
         vmem((16, 128), F32),
         vmem((3, 8, 256), F32),
@@ -725,7 +883,6 @@
         vmem((12, 8, 128), F32),
         pltpu.SemaphoreType.DMA((COUNT,)),
         pltpu.SemaphoreType.DMA((COUNT,)),
-        pltpu.SemaphoreType.DMA((3,)),
     ]
     whole_vmem = pl.BlockSpec(memory_space=pltpu.VMEM)
     return pl.pallas_call(
@@ -736,14 +893,14 @@
             jax.ShapeDtypeStruct((32, SLAB), F32),
             jax.ShapeDtypeStruct((24, 128), F32),
         ),
-        in_specs=[whole_vmem] * 5 + [pl.BlockSpec(memory_space=pltpu.SMEM)],
+        in_specs=[whole_vmem] * len(operands),
         out_specs=(whole_vmem,) * 4,
         scratch_shapes=scratch,
         compiler_params=pltpu.CompilerParams(
             collective_id=0, has_side_effects=True, vmem_limit_bytes=60 << 20
         ),
         name="layer",
-    )(slab, small, hidden, cot, starts, slope)
+    )(*operands)
 
 
 def on_device(
@@ -761,32 +918,19 @@
     cotangent,
 ):
     f, k, t = lax.axis_index("fsdp"), lax.axis_index("ctx"), lax.axis_index("tp")
-    slope = jnp.exp2(-8.0 * (t * 4 + k + 1).astype(F32) / H).reshape(1, 1)
-    segments = segment_ids[0]
-    starts = jnp.zeros((2048,), jnp.int32)
-    for value in range(1, 4):
-        starts = jnp.where(
-            segments >= value, jnp.sum((segments < value).astype(jnp.int32)), starts
-        )
-    starts = starts.reshape(1, 2048)
-
-    qkv_cols = w_qkv[0].reshape(3, 32, 4, 64).transpose(1, 2, 0, 3).reshape(32, 768)
-    slab = jnp.concatenate([w_up[0], w_down[0], qkv_cols, w_out[0]], axis=1)
-
-    norms = jnp.concatenate([norm_gain[0], norm_bias[0], out_bias[0], jnp.zeros((2, 8), F32)])
-    lane = jnp.arange(128, dtype=jnp.int32)
-    norms = jnp.where(lane[None] // 8 == k * 4 + t, jnp.tile(norms, (1, 16)), 0.0)
-    qv = qv_bias[0].astype(F32)
-    qv = jnp.where(lane[None, None, :64] // 2 == f * 4 + k, jnp.tile(qv, (1, 1, 32)), 0.0)
-    qkv_bias = jnp.stack([qv[0], jnp.zeros_like(qv[0]), qv[1]], axis=1).reshape(6, 128)
-    lane = jnp.arange(256, dtype=jnp.int32)
-    up = jnp.where(
-        lane[None] // 8 == f * 4 + k, jnp.tile(up_bias[0].astype(F32), (1, 32)), 0.0
-    ).reshape(8, 128)
-    small = jnp.concatenate([norms, qkv_bias, up, jnp.zeros((2, 128), F32)])
-
     hidden_out, grad_input, out, sums = run_layer(
-        slab, small, hidden_in, cotangent, starts, slope
+        w_up,
+        w_down,
+        w_qkv,
+        w_out,
+        norm_gain,
+        norm_bias,
+        out_bias,
+        qv_bias,
+        up_bias,
+        hidden_in,
+        cotangent,
+        segment_ids,
     )
 
     norm_sums = lax.dynamic_slice_in_dim(sums[0:6], (k * 4 + t) * 8, 8, 1)

time: 185 us -> 171 us (0.924)
  Pallas kernels: 165 us -> 160 us
  other arithmetic: 4.96 us -> 0.08 us
  local copies, waits for them, and re-layouts: 13.2 us -> 10.1 us
    pallas_call x1, Pallas kernels: 165 us -> 160 us  [run_layer(): pl.pallas_call(layer_kernel, out_shape=(jax.ShapeDtypeStruct((128, 1024),...]
    select_n x3 -> x0, other arithmetic: 2.63 us -> none  [the longest x1 2.55 us: on_device(): jnp.where(segments >= value, jnp.sum((segments < value).astype(jnp.int32)...]
    unnamed x26 -> x9, local copies, waits for them, and re-layouts: 4.71 us -> 3.39 us
where the time goes in v2:
time: 171 us
  Pallas kernels  160 us (94%)
  local copies, waits for them, and re-layouts  10.1 us (6%)
    pallas_call x1, Pallas kernels, run_layer(): pl.pallas_call(layer_kernel, out_shape=(jax.ShapeDtypeStruct((128, 1024),...  160 us

profile of v2, /device:TPU:1, one launch (start us, length us, event | category | flops | bytes accessed | tf_op | source)
XLA Modules:
  0.0 170.6 jit_solution(5111408073110951903)
XLA Ops:
  0.6 1.4 copy.30.qv_in
  2.0 159.7 %layer.1 = (f32[128,1024]{1,0:T(8,128)}, f32[128,1024]{1,0:T(8,128)}, f32[32,3072]{1,0:T(8,128)}, f32[24,128]{1,0:T(8,128)}) custom-call(bf16[1,32,1024]{2,1,0:T(8,128)(2,1)} %w_up.1, bf16[1,32,1024]{2,1,0:T(8,128)(2,1)} %w_down.1, bf16[1,3,32,256]{3,2,1,0:T(8,128)(2,1)} %w_qkv.1, bf16[1,32,256]{2,1,0:T(8,128)(2,1)} %w_out.1, f32[1,2,8]{2,1,0:T(2,128)} %gain_in.1, ...), custom_call_target="tpu_custom_call" | custom-call | tf_op jit(solution)/shard_map/layer/pallas_call | solution.py:888
  161.7 0.7 fusion
  162.4 0.1 constant_dynamic-slice_fusion
  162.5 0.6 slice_bitcast_fusion.3
  163.1 0.9 slice.39
  164.0 0.1 reshape.60
  164.1 0.0 copy-start.2
  164.1 0.1 copy.31
  164.2 0.0 copy-start.1
  164.2 0.8 reshape.61
  165.0 0.1 reshape.62
  165.1 0.1 dynamic-slice_maximum_fusion
  165.2 0.7 copy.33
  165.9 0.0 copy-done.2
  165.9 0.6 slice_bitcast_fusion.2
  166.5 0.7 slice_bitcast_fusion
  167.2 0.7 slice.46
  167.9 0.6 dynamic-slice_bitcast_fusion
  168.6 0.0 copy-done.1
  168.6 0.0 copy-start
  168.6 0.8 copy.37
  169.4 0.4 copy-done
  169.8 0.8 copy.38
  (2 shorter events, 0.0 us)
Async XLA Ops:
  164.1 1.7 %copy-start.2 = (f32[32,3072]{1,0:T(8,128)S(1)}, f32[32,3072]{1,0:T(8,128)}, u32[]{:S(2)}) copy-start(f32[32,3072]{1,0:T(8,128)} %get-tuple-element.18) | copy-start | bytes 1179652
  164.2 4.4 %copy-start.1 = (f32[128,1024]{1,0:T(8,128)S(1)}, f32[128,1024]{1,0:T(8,128)}, u32[]{:S(2)}) copy-start(f32[128,1024]{1,0:T(8,128)} %get-tuple-element.39) | copy-start | bytes 1572868
  168.6 1.2 copy-start

commit v3 on v2

--- a/solution.py
+++ b/solution.py
@@ -79,21 +79,35 @@
 def layer_kernel(
     w_up,
     w_down,
-    w_qkv,
+    w_qkv_hbm,
     w_out,
     gain_in,
     shift_in,
     obias_in,
     qv_in,
     ub_in,
+    hidden_hbm,
+    cot_hbm,
+    segments,
+    r2_hbm,
+    g0_hbm,
+    qkv_hbm,
+    out_hbm,
+    up_hbm,
+    down_hbm,
+    gain_out,
+    shift_out,
+    obias_out,
+    qv_out,
+    ub_out,
+    whole,
+    w_qkv,
     hidden,
     cot,
-    segments,
     r2_out,
     g0_out,
     slab_out,
-    small_out,
-    whole,
+    slab_qkv,
     small,
     starts,
     near_c,
@@ -171,6 +185,7 @@
     sg_x,
     send_sems,
     recv_sems,
+    local_sems,
 ):
     f, k, t = lax.axis_index("fsdp"), lax.axis_index("ctx"), lax.axis_index("tp")
     z, yh = f // 2, lax.rem(f, 2)
@@ -193,6 +208,21 @@
 
     def member(dt, dk):
         return (f, around(k, dk), around(t, dt))
+
+    def move(index, src, dst):
+        copy = pltpu.make_async_copy(src, dst, local_sems.at[index])
+        copy.start()
+        return copy
+
+    own_out = pl.ds(pl.multiple_of(2816 + t * 256, 256), 256)
+    qkv_load = move(0, w_qkv_hbm, w_qkv)
+    out_load = move(1, w_out.at[0], whole.at[z, y, c, :, own_out])
+    hidden_load = move(2, hidden_hbm, hidden)
+    mlp_loads = [
+        move(3, w_up.at[0], whole.at[z, y, c, :, 768:1792]),
+        move(4, w_down.at[0], whole.at[z, y, c, :, 1792:2816]),
+    ]
+    cot_load = move(5, cot_hbm, cot)
 
     barrier = pltpu.get_barrier_semaphore()
     greeted = [member(dt, dk) for dt, dk in group] + y_peers + z_peers
@@ -328,18 +358,17 @@
         yield
         arrived(core)
 
+    qkv_load.wait()
     for j in range(4):
         for i in range(3):
             col = j * 192 + i * 64
             whole[z, y, c, :, col : col + 64] = w_qkv[0, i, :, j * 64 : j * 64 + 64]
     gather_qkv = gather(QKV)
     step(gather_qkv)
-    own_out = pl.ds(pl.multiple_of(2816 + t * 256, 256), 256)
-    whole[z, y, c, :, own_out] = w_out[0]
+    out_load.wait()
     out_cols = whole.at[z, y, c, :, own_out]
     out_x = [make(out_cols, out_cols, peer) for peer in tp_peers]
-    whole[z, y, c, :, 768:1792] = w_up[0]
-    whole[z, y, c, :, 1792:2816] = w_down[0]
+    hidden_load.wait()
 
     r = hidden[...].astype(F32)
     centered = r - row_mean(r)
@@ -387,6 +416,7 @@
     gather_out = gather(OUT)
     step(gather_out)
     wide1_x = wide1_x()
+    cot_load.wait()
     gwide[t] = cot[...].astype(BF16)
     ids = segments[...]
     first = jnp.zeros((1, 2048), F32)
@@ -416,11 +446,13 @@
     ]
     qkv_in[k] = qkv_out[head_rows(k)]
     step(gather_out)
-    gather_mlp = gather(MLP)
-    step(gather_mlp)
     gwide_x = gwide_x()
     step(gather_out)
     arrived(heads_c)
+    for copy in mlp_loads:
+        copy.wait()
+    gather_mlp = gather(MLP)
+    step(gather_mlp)
     for i in range(4):
         span = slice(i * 512, (i + 1) * 512)
         q_t[:, span] = qkv_in[i, 0:64]
@@ -733,6 +765,7 @@
     reduce_out = reduce(2)
     step(reduce_out, reduce_up, reduce_down)
     r2_out[...] = r1[...] + sum_rows(part_dn, in_dn) + vec[5:6]
+    stores = [move(6, r2_out, r2_hbm)]
     arrived(back_c)
     gqkv[...] = gqkv_in[...].reshape(768, 512).T
     sum_g1 = ring_sum_rows(part_g1, via_g1, in_g1, partial_rows(gqkv, QKV, part_g1))
@@ -765,6 +798,7 @@
     ] + [make(tsum, sz_tp.at[d - 1], z_peers[d - 1]) for d in STEPS]
     step(reduce_qkv, reduce_out)
     g0_out[...] = g1[...] + norm_back(total, unit1[...], inv1[...], vec[0:1])
+    stores.append(move(7, g0_out, g0_hbm))
     arrived(sum_z)
     v1[...] = (
         vsum[:, pl.ds(pl.multiple_of(z * 256, 256), 256)] + sz_vec[0] + sz_vec[1] + sz_vec[2]
@@ -784,17 +818,80 @@
     step(reduce_qkv, reduce_out)
     step(reduce_qkv, reduce_out)
     step(reduce_up, reduce_down)
+    for j in range(4):
+        for i in range(3):
+            col = 2048 + j * 192 + i * 64
+            slab_qkv[0, i, :, j * 64 : j * 64 + 64] = slab_out[:, col : col + 64]
+    stores += [
+        move(8, slab_qkv, qkv_hbm),
+        move(9, slab_out.at[:, 2816:3072], out_hbm.at[0]),
+        move(10, slab_out.at[:, 0:1024], up_hbm.at[0]),
+        move(11, slab_out.at[:, 1024:2048], down_hbm.at[0]),
+    ]
     arrived(sum_c)
     arrived(sum_x)
     total = s_g[...] + sg_c[0] + sg_c[1] + sg_c[2]
     norms = total[0:8]
     for i in range(12):
         norms = norms + sg_x[i]
-    small_out[0:8] = norms
-    small_out[8:24] = total[8:24]
+    def pick(values, hot):
+        return lax.dot_general(
+            values, hot, NT, precision=lax.Precision.HIGHEST, preferred_element_type=F32
+        )
+
+    mine = pick(norms, own)
+    gain_out[0] = mine[0:2]
+    shift_out[0] = mine[2:4]
+    obias_out[0] = mine[4:6]
+    left = lax.broadcasted_iota(jnp.int32, (2, 128), 1) < 64
+    from_left = pick(total[8:24], jnp.where(left, pair, 0.0))
+    from_right = pick(total[8:24], jnp.where(left, 0.0, pair))
+    qv_out[0, 0, 0:1] = from_left[0:1]
+    qv_out[0, 0, 1:2] = from_right[1:2]
+    qv_out[0, 0, 2:3] = from_left[3:4]
+    qv_out[0, 0, 3:4] = from_right[4:5]
+    qv_out[0, 1, 0:1] = from_left[1:2]
+    qv_out[0, 1, 1:2] = from_right[2:3]
+    qv_out[0, 1, 2:3] = from_left[4:5]
+    qv_out[0, 1, 3:4] = from_right[5:6]
+    ups = pick(total[8:24], lanes(8, 128, lax.rem(place, 16)))
+    for i in range(4):
+        ub_out[0, i : i + 1] = (
+            ups[6 + 2 * i : 7 + 2 * i] * even + ups[7 + 2 * i : 8 + 2 * i] * (1.0 - even)
+        )
+    for copy in stores:
+        copy.wait()
     copies.finish()
 
 
+def place_kernel(*refs):
+    count = (len(refs) - 1) // 2
+    sems = refs[-1]
+    copies = []
+    for i, (src, dst) in enumerate(zip(refs[:count], refs[count : 2 * count])):
+        if i < 6:
+            copy = pltpu.make_async_copy(src, dst, sems.at[i])
+            copy.start()
+            copies.append(copy)
+        else:
+            dst[...] = src[...]
+    for copy in copies:
+        copy.wait()
+
+
+OUTPUTS = (
+    (128, 1024),
+    (128, 1024),
+    (1, 3, 32, 256),
+    (1, 32, 256),
+    (1, 32, 1024),
+    (1, 32, 1024),
+    (1, 2, 8),
+    (1, 2, 8),
+    (1, 2, 8),
+    (1, 2, 4, 2),
+    (1, 4, 8),
+)
 COUNT = 336
 
 
@@ -806,6 +903,13 @@
 
     scratch = [
         vmem((4, 4, 2, 32, WIDE), BF16),
+        vmem((1, 3, 32, 256), BF16),
+        vmem((128, 1024), BF16),
+        vmem((128, 1024), F32),
+        vmem((128, 1024), F32),
+        vmem((128, 1024), F32),
+        vmem((32, SLAB), F32),
+        vmem((1, 3, 32, 256), F32),
         vmem((24, 128), F32),
         vmem((1, 2048), F32),
         vmem((3, 24, 128), F32),
@@ -883,24 +987,30 @@
         vmem((12, 8, 128), F32),
         pltpu.SemaphoreType.DMA((COUNT,)),
         pltpu.SemaphoreType.DMA((COUNT,)),
+        pltpu.SemaphoreType.DMA((12,)),
     ]
-    whole_vmem = pl.BlockSpec(memory_space=pltpu.VMEM)
-    return pl.pallas_call(
+    in_vmem, in_place = pl.BlockSpec(memory_space=pltpu.VMEM), pl.BlockSpec(memory_space=pl.ANY)
+    shapes = tuple(jax.ShapeDtypeStruct(shape, F32) for shape in OUTPUTS)
+    places = (in_place,) * 6 + (in_vmem,) * 5
+    results = pl.pallas_call(
         layer_kernel,
-        out_shape=(
-            jax.ShapeDtypeStruct((128, 1024), F32),
-            jax.ShapeDtypeStruct((128, 1024), F32),
-            jax.ShapeDtypeStruct((32, SLAB), F32),
-            jax.ShapeDtypeStruct((24, 128), F32),
-        ),
-        in_specs=[whole_vmem] * len(operands),
-        out_specs=(whole_vmem,) * 4,
+        out_shape=shapes,
+        in_specs=[in_place] * 4 + [in_vmem] * 5 + [in_place] * 2 + [in_vmem],
+        out_specs=places,
         scratch_shapes=scratch,
         compiler_params=pltpu.CompilerParams(
             collective_id=0, has_side_effects=True, vmem_limit_bytes=60 << 20
         ),
         name="layer",
     )(*operands)
+    return pl.pallas_call(
+        place_kernel,
+        out_shape=shapes,
+        in_specs=list(places),
+        out_specs=places,
+        scratch_shapes=[pltpu.SemaphoreType.DMA((6,))],
+        name="place",
+    )(*results)
 
 
 def on_device(
@@ -917,8 +1027,7 @@
     w_down,
     cotangent,
 ):
-    f, k, t = lax.axis_index("fsdp"), lax.axis_index("ctx"), lax.axis_index("tp")
-    hidden_out, grad_input, out, sums = run_layer(
+    hidden_out, grad_input, qkv, out, up, down, gain, shift, obias, qv, ub = run_layer(
         w_up,
         w_down,
         w_qkv,
@@ -932,26 +1041,7 @@
         cotangent,
         segment_ids,
     )
-
-    norm_sums = lax.dynamic_slice_in_dim(sums[0:6], (k * 4 + t) * 8, 8, 1)
-    qkv_sums = sums[8:14].reshape(4, 3, 64)
-    qv_sums = lax.dynamic_slice_in_dim(
-        jnp.stack([qkv_sums[:, 0], qkv_sums[:, 2]]), (f * 4 + k) * 2, 2, 2
-    )
-    up_sums = lax.dynamic_slice_in_dim(sums[14:22].reshape(4, 256), (f * 4 + k) * 8, 8, 1)
-    return (
-        hidden_out,
-        grad_input,
-        norm_sums[0:2].reshape(1, 2, 8),
-        norm_sums[2:4].reshape(1, 2, 8),
-        out[:, 2048:2816].reshape(32, 4, 3, 64).transpose(2, 0, 1, 3).reshape(1, 3, 32, 256),
-        qv_sums.reshape(1, 2, 4, 2),
-        out[:, 2816:3072].reshape(1, 32, 256),
-        norm_sums[4:6].reshape(1, 2, 8),
-        out[:, 0:1024].reshape(1, 32, 1024),
-        up_sums.reshape(1, 4, 8),
-        out[:, 1024:2048].reshape(1, 32, 1024),
-    )
+    return hidden_out, grad_input, gain, shift, qkv, qv, out, obias, up, ub, down
 
 
 def solution(mesh):

time: 171 us -> 209 us (1.22)
  Pallas kernels: 160 us -> 205 us
  local copies, waits for them, and re-layouts: 10.1 us -> 2.69 us
    pallas_call x1 -> x2, Pallas kernels: 160 us -> 205 us  [the longest x1 159 us: run_layer(): pl.pallas_call(layer_kernel, out_shape=shapes, in_specs=[in_place] * 4 +...]
    reshape x8 -> x0, local copies, waits for them, and re-layouts: 3.6 us -> none  [the longest x2 0.95 us: on_device(): out[:, 2048:2816].reshape(32, 4, 3, 64).transpose(2, 0, 1, 3)]
    slice x4 -> x0, local copies, waits for them, and re-layouts: 2.29 us -> none  [the longest x1 0.9 us: on_device(): out[:, 2048:2816].reshape(32, 4, 3, 64).transpose(2, 0, 1, 3)]
where the time goes in v3:
time: 209 us
  Pallas kernels  205 us (98%)
  local copies, waits for them, and re-layouts  2.69 us (1%)
    pallas_call x1, Pallas kernels, run_layer(): pl.pallas_call(layer_kernel, out_shape=shapes, in_specs=[in_place] * 4 +...  159 us
    pallas_call x1, Pallas kernels, run_layer(): pl.pallas_call(place_kernel, out_shape=shapes, in_specs=list(places), out...  46.1 us

profile of v3, /device:TPU:1, one launch (start us, length us, event | category | flops | bytes accessed | tf_op | source)
XLA Modules:
  0.0 208.8 jit_solution(5063485736691468699)
XLA Ops:
  0.6 1.4 copy.23.qv_in
  2.0 159.3 %layer.1 = (f32[128,1024]{1,0:T(8,128)}, f32[128,1024]{1,0:T(8,128)}, f32[1,3,32,256]{3,2,1,0:T(8,128)}, f32[1,32,256]{2,1,0:T(8,128)}, f32[1,32,1024]{2,1,0:T(8...) custom-call(bf16[1,32,1024]{2,1,0:T(8,128)(2,1)} %w_up.1, ...), custom_call_target="tpu_custom_call" | custom-call | tf_op jit(solution)/shard_map/layer/pallas_call | solution.py:995
  161.3 46.1 %place.1 = (f32[128,1024]{1,0:T(8,128)}, f32[128,1024]{1,0:T(8,128)}, f32[1,3,32,256]{3,2,1,0:T(8,128)}, f32[1,32,256]{2,1,0:T(8,128)}, f32[1,32,1024]{2,1,0:T(8...) custom-call(f32[128,1024]{1,0:T(8,128)} %get-tuple-element.33.refs_0, ...), custom_call_target="tpu_custom_call" | custom-call | tf_op jit(solution)/shard_map/place/pallas_call | solution.py:1006
  207.5 0.0 copy-start
  207.5 0.7 copy-done
  208.1 0.7 copy.24
Async XLA Ops:
  207.5 0.7 copy-start

commit v4 on v3

--- a/solution.py
+++ b/solution.py
@@ -113,13 +113,12 @@
     near_c,
     near_x,
     tile_own,
-    tile_z,
-    pack_y,
-    pack_yin,
+    tile_f,
     vec,
     bias_q,
     bias_u,
     wide1,
+    normed1,
     gwide,
     wide2,
     gawide,
@@ -174,12 +173,8 @@
     b_last,
     vsum,
     tsum,
-    sz_vec,
-    sz_tp,
-    v1,
-    t1,
-    s_y,
-    s_yin,
+    s_out,
+    s_in,
     s_g,
     sg_c,
     sg_x,
@@ -201,8 +196,8 @@
     y_peers = [at_zy(z, around(y, d), c) for d in STEPS]
     z_peers = [at_zy(around(z, d), y, c) for d in STEPS]
     sibling = at_zy(z, y, 1 - c)
-    opposite = at_zy(z, around(y, 2), c)
     ctx_peers = [(f, around(k, d), t) for d in STEPS]
+    fsdp_peers = [(lax.rem(f + d, 8), k, t) for d in range(1, 8)]
     tp_peers = [(f, k, around(t, d)) for d in STEPS]
     group = [(dt, dk) for dt in range(4) for dk in range(4) if (dt, dk) != (0, 0)]
 
@@ -225,12 +220,9 @@
     cot_load = move(5, cot_hbm, cot)
 
     barrier = pltpu.get_barrier_semaphore()
-    greeted = [member(dt, dk) for dt, dk in group] + y_peers + z_peers
+    greeted = [member(dt, dk) for dt, dk in group] + y_peers + fsdp_peers
     for partner in greeted:
         pl.semaphore_signal(barrier, inc=1, device_id=partner, device_id_type=MESH)
-    pl.semaphore_wait(barrier, len(greeted))
-    copies = Copies(send_sems, recv_sems)
-    make = copies.make
 
     def lanes(count, period, index):
         row = lax.broadcasted_iota(jnp.int32, (count, 128), 0)
@@ -263,6 +255,24 @@
     for i in range(4):
         small[14 + 2 * i : 15 + 2 * i] = up_row[i : i + 1] * even
         small[15 + 2 * i : 16 + 2 * i] = up_row[i : i + 1] * (1.0 - even)
+    qkv_load.wait()
+    for j in range(4):
+        for i in range(3):
+            col = j * 192 + i * 64
+            whole[z, y, c, :, col : col + 64] = w_qkv[0, i, :, j * 64 : j * 64 + 64]
+
+    hidden_load.wait()
+    r = hidden[...].astype(F32)
+    centered = r - row_mean(r)
+    rstd = lax.rsqrt(row_mean(centered * centered) + EPS)
+    unit1[...] = centered * rstd
+    inv1[...] = rstd
+    wide1[t] = unit1[...].astype(BF16)
+    out_load.wait()
+
+    pl.semaphore_wait(barrier, len(greeted))
+    copies = Copies(send_sems, recv_sems)
+    make = copies.make
     small_c = [make(small, near_c.at[d - 1], ctx_peers[d - 1]) for d in STEPS]
     far = [(dt, dk) for dt, dk in group if dt]
     small_x = [
@@ -358,23 +368,11 @@
         yield
         arrived(core)
 
-    qkv_load.wait()
-    for j in range(4):
-        for i in range(3):
-            col = j * 192 + i * 64
-            whole[z, y, c, :, col : col + 64] = w_qkv[0, i, :, j * 64 : j * 64 + 64]
     gather_qkv = gather(QKV)
     step(gather_qkv)
-    out_load.wait()
+    wide1_x = ring_rows(wide1)
     out_cols = whole.at[z, y, c, :, own_out]
     out_x = [make(out_cols, out_cols, peer) for peer in tp_peers]
-    hidden_load.wait()
-
-    r = hidden[...].astype(F32)
-    centered = r - row_mean(r)
-    rstd = lax.rsqrt(row_mean(centered * centered) + EPS)
-    unit1[...] = centered * rstd
-    inv1[...] = rstd
 
     arrived(small_c)
     arrived(small_x)
@@ -384,38 +382,21 @@
         norms = norms + near_x[i]
     tile_own[0:8] = norms
     tile_own[8:24] = total[8:24]
-    small_z = [make(tile_own, tile_z.at[d - 1], z_peers[d - 1]) for d in STEPS]
+    small_f = [make(tile_own, tile_f.at[d], fsdp_peers[d]) for d in range(7)]
     step(gather_qkv)
-    arrived(small_z)
-    pack_y[0] = tile_own[0:8]
+    wide1_x = wide1_x()
+    step(gather_qkv)
+    arrived(small_f)
+    vec[:, pl.ds(pl.multiple_of(f * 128, 128), 128)] = tile_own[0:8]
     columns = tile_own[8:24]
-    for d in STEPS:
-        pack_y[d] = tile_z[d - 1, 0:8]
-        columns = columns + tile_z[d - 1, 8:24]
-    pack_y[4] = columns[0:8]
-    pack_y[5] = columns[8:16]
-    small_y = make(pack_y, pack_yin, opposite)
-    step(gather_qkv)
-    small_y.wait_recv()
-    for d in range(4):
-        origin = around(z, 4 - d) * 2
-        vec[:, pl.ds(pl.multiple_of((origin + yh) * 128, 128), 128)] = pack_y[d]
-        vec[:, pl.ds(pl.multiple_of((origin + 1 - yh) * 128, 128), 128)] = pack_yin[d]
-    first_rows = pack_y[4] + pack_yin[4]
-    later_rows = pack_y[5] + pack_yin[5]
-    rows = [first_rows[i : i + 1] for i in range(8)] + [later_rows[i : i + 1] for i in range(6)]
+    for d in range(7):
+        origin = lax.rem(f + 7 - d, 8)
+        vec[:, pl.ds(pl.multiple_of(origin * 128, 128), 128)] = tile_f[d, 0:8]
+        columns = columns + tile_f[d, 8:24]
     for i in range(6):
-        bias_q[:, i * 128 : (i + 1) * 128] = rows[i]
+        bias_q[:, i * 128 : (i + 1) * 128] = columns[i : i + 1]
     for i in range(8):
-        bias_u[:, i * 128 : (i + 1) * 128] = rows[6 + i]
-
-    wide1[t] = (unit1[...] * vec[0:1] + vec[2:3]).astype(BF16)
-    wide1_x = ring_rows(wide1)
-    step(gather_qkv)
-    arrived(out_x)
-    gather_out = gather(OUT)
-    step(gather_out)
-    wide1_x = wide1_x()
+        bias_u[:, i * 128 : (i + 1) * 128] = columns[6 + i : 7 + i]
     cot_load.wait()
     gwide[t] = cot[...].astype(BF16)
     ids = segments[...]
@@ -425,14 +406,20 @@
         first = jnp.where(ids >= value, count, first)
     starts[...] = first
     step(gather_qkv)
+    arrived(out_x)
+    gather_out = gather(OUT)
+    step(gather_out)
+    arrived(wide1_x)
+    gwide_x = ring_rows(gwide)
+    for i in range(4):
+        normed1[i] = (wide1[i].astype(F32) * vec[0:1] + vec[2:3]).astype(BF16)
+    step(gather_qkv)
     step(gather_out)
     step(gather_qkv)
-    arrived(wide1_x)
-    gwide_x = ring_rows(gwide)
 
     def project(n, carry):
         cols = pl.ds(pl.multiple_of(n * 256, 256), 256)
-        out = dot(wide1[...].reshape(512, 1024), whole[:, :, :, :, cols].reshape(1024, 256))
+        out = dot(normed1[...].reshape(512, 1024), whole[:, :, :, :, cols].reshape(1024, 256))
         qkv_out[cols] = (out + bias_q[:, cols]).T.astype(BF16)
         return carry
 
@@ -777,7 +764,7 @@
     for i in range(8):
         tsum[6 + i : 7 + i] = bias_u[:, i * 128 : (i + 1) * 128]
     tsum[14:16] = jnp.zeros((2, 128), F32)
-    matrix_grad(wide1, gqkv, 3)
+    matrix_grad(normed1, gqkv, 3)
     reduce_qkv = reduce(3)
     step(reduce_qkv, sum_g1, reduce_out)
 
@@ -788,29 +775,21 @@
     vsum[0:1] = jnp.sum(total * unit1[...], axis=0, keepdims=True)
     vsum[2:3] = jnp.sum(total, axis=0, keepdims=True)
     vsum[6:8] = jnp.zeros((2, 1024), F32)
-    sum_z = [
-        make(
-            vsum.at[:, pl.ds(pl.multiple_of(around(z, d) * 256, 256), 256)],
-            sz_vec.at[d - 1],
-            z_peers[d - 1],
-        )
-        for d in STEPS
-    ] + [make(tsum, sz_tp.at[d - 1], z_peers[d - 1]) for d in STEPS]
+    for i in range(8):
+        s_out[i, 0:8] = vsum[:, i * 128 : (i + 1) * 128]
+        s_out[i, 8:24] = tsum[...]
+    sum_f = [
+        make(s_out.at[lax.rem(f + d + 1, 8)], s_in.at[d], fsdp_peers[d]) for d in range(7)
+    ]
     step(reduce_qkv, reduce_out)
     g0_out[...] = g1[...] + norm_back(total, unit1[...], inv1[...], vec[0:1])
     stores.append(move(7, g0_out, g0_hbm))
-    arrived(sum_z)
-    v1[...] = (
-        vsum[:, pl.ds(pl.multiple_of(z * 256, 256), 256)] + sz_vec[0] + sz_vec[1] + sz_vec[2]
-    )
-    t1[...] = tsum[...] + sz_tp[0] + sz_tp[1] + sz_tp[2]
-    s_y[0:8] = v1[:, pl.ds(pl.multiple_of((1 - yh) * 128, 128), 128)]
-    s_y[8:24] = t1[...]
-    sum_y = make(s_y, s_yin, opposite)
     step(reduce_qkv, reduce_out)
-    sum_y.wait_recv()
-    s_g[0:8] = v1[:, pl.ds(pl.multiple_of(yh * 128, 128), 128)] + s_yin[0:8]
-    s_g[8:24] = t1[...] + s_yin[8:24]
+    arrived(sum_f)
+    total = s_out[f]
+    for d in range(7):
+        total = total + s_in[d]
+    s_g[...] = total
     sum_c = [make(s_g, sg_c.at[d - 1], ctx_peers[d - 1]) for d in STEPS]
     sum_x = [
         make(s_g.at[pl.ds(0, 8)], sg_x.at[i], member(dt, dk)) for i, (dt, dk) in enumerate(far)
@@ -865,18 +844,9 @@
 
 
 def place_kernel(*refs):
-    count = (len(refs) - 1) // 2
-    sems = refs[-1]
-    copies = []
-    for i, (src, dst) in enumerate(zip(refs[:count], refs[count : 2 * count])):
-        if i < 6:
-            copy = pltpu.make_async_copy(src, dst, sems.at[i])
-            copy.start()
-            copies.append(copy)
-        else:
-            dst[...] = src[...]
-    for copy in copies:
-        copy.wait()
+    count = len(refs) // 2
+    for src, dst in zip(refs[:count], refs[count:]):
+        dst[...] = src[...]
 
 
 OUTPUTS = (
@@ -915,12 +885,11 @@
         vmem((3, 24, 128), F32),
         vmem((12, 8, 128), F32),
         vmem((24, 128), F32),
-        vmem((3, 24, 128), F32),
-        vmem((6, 8, 128), F32),
-        vmem((6, 8, 128), F32),
+        vmem((7, 24, 128), F32),
         vmem((8, 1024), F32),
         vmem((1, 768), F32),
         vmem((1, 1024), F32),
+        vmem((4, 128, 1024), BF16),
         vmem((4, 128, 1024), BF16),
         vmem((4, 128, 1024), BF16),
         vmem((4, 128, 1024), BF16),
@@ -976,12 +945,8 @@
         per_chunk(2, 16),
         vmem((8, 1024), F32),
         vmem((16, 128), F32),
-        vmem((3, 8, 256), F32),
-        vmem((3, 16, 128), F32),
-        vmem((8, 256), F32),
-        vmem((16, 128), F32),
-        vmem((24, 128), F32),
-        vmem((24, 128), F32),
+        vmem((8, 24, 128), F32),
+        vmem((7, 24, 128), F32),
         vmem((24, 128), F32),
         vmem((3, 24, 128), F32),
         vmem((12, 8, 128), F32),
@@ -1006,9 +971,8 @@
     return pl.pallas_call(
         place_kernel,
         out_shape=shapes,
-        in_specs=list(places),
-        out_specs=places,
-        scratch_shapes=[pltpu.SemaphoreType.DMA((6,))],
+        in_specs=[in_vmem] * len(shapes),
+        out_specs=(in_vmem,) * len(shapes),
         name="place",
     )(*results)
 

time: 209 us -> 161 us (0.77)
  Pallas kernels: 205 us -> 156 us
    pallas_call x1, Pallas kernels: 46.1 us -> 2.47 us  [run_layer(): pl.pallas_call(place_kernel, out_shape=shapes, in_specs=[in_vmem] * len(s...]
    pallas_call x1, Pallas kernels: 159 us -> 154 us  [run_layer(): pl.pallas_call(layer_kernel, out_shape=shapes, in_specs=[in_place] * 4 +...]
where the time goes in v4:
time: 161 us; the launch traced here: 160 us
  Pallas kernels  156 us (97%)
  local copies, waits for them, and re-layouts  2.69 us (2%)
    pallas_call x1, Pallas kernels, run_layer(): pl.pallas_call(layer_kernel, out_shape=shapes, in_specs=[in_place] * 4 +...  154 us

profile of v4, /device:TPU:1, one launch (start us, length us, event | category | flops | bytes accessed | tf_op | source)
XLA Modules:
  0.0 159.8 jit_solution(12770300757526399210)
XLA Ops:
  0.6 1.4 copy.23.qv_in
  2.0 153.9 %layer.1 = (f32[128,1024]{1,0:T(8,128)}, f32[128,1024]{1,0:T(8,128)}, f32[1,3,32,256]{3,2,1,0:T(8,128)}, f32[1,32,256]{2,1,0:T(8,128)}, f32[1,32,1024]{2,1,0:T(8...) custom-call(bf16[1,32,1024]{2,1,0:T(8,128)(2,1)} %w_up.1, ...), custom_call_target="tpu_custom_call" | custom-call | tf_op jit(solution)/shard_map/layer/pallas_call | solution.py:960
  155.9 2.5 %place.1 = (f32[128,1024]{1,0:T(8,128)}, f32[128,1024]{1,0:T(8,128)}, f32[1,3,32,256]{3,2,1,0:T(8,128)}, f32[1,32,256]{2,1,0:T(8,128)}, f32[1,32,1024]{2,1,0:T(8...) custom-call(f32[128,1024]{1,0:T(8,128)} %get-tuple-element.33.refs_0, ...), custom_call_target="tpu_custom_call" | custom-call | tf_op jit(solution)/shard_map/place/pallas_call | solution.py:971
  158.4 0.0 copy-start
  158.4 0.7 copy-done
  159.1 0.7 copy.24
Async XLA Ops:
  158.4 0.7 copy-start
